TPU v7x, 32 devices: a whole 2x2x4 slice. The times are simulated.
32 devices in a mesh: space: 8 (over z, y), rep: 4 (over x, core).
Axes of the slice: x: 2, y: 2, z: 4, core: 2. Of those that a mesh axis runs over, the one named last changes fastest.
Arguments:
- features: bfloat16 [128, 64, 512], P(('space', 'rep')), may hold values from -6 to 6
- neighbours: int32 [128, 27], P(('space', 'rep')), may hold values from -1 to 7, as said below
- counts: int32 [32], P(('space', 'rep')), may hold values from 1 to 4, as said below
- cotangent: bfloat16 [128, 64, 128], P(('space', 'rep')), may hold values from -0.06591797 to 0.06591797
- conv_weight: bfloat16 [27, 64, 64], replicated, may hold values from -0.15625 to 0.15625
- down_weight: bfloat16 [8, 128, 64], replicated, may hold values from -0.25 to 0.25
Outputs:
- hidden: bfloat16 [128, 64, 512], P(('space', 'rep'))
- conv_grad: float32 [27, 64, 64], replicated
- down_grad: float32 [8, 128, 64], replicated
Inputs may be any that keep to these rules, and one draw needn't show every extreme that they name: `counts`: in every tile, of the two strips s and s + 4 at most one has more than 2 occupied blocks; some strip has exactly 4 and some exactly 2. Only live slots name neighbours, and they name only live slots; strip 0 names nothing below and the last strip nothing above.
All inputs are finite; a program needn't handle non-finite values.
Results may differ from a plain program's by a relative error of at most 0.0029.
Values may be sent and summed in bfloat16 or wider, within the bound.
No kernel may reach another device: no remote copies, remote signals or barrier semaphores. Data moves between devices by JAX's collectives and lax.ppermute only.
A program may use at most 64 MiB of HBM per device.

v0:
```python
import jax
import jax.numpy as jnp
from jax import lax
from jax.sharding import PartitionSpec as P


def from_behind(block, axis, distance):
    devices = range(lax.axis_size(axis))
    route = [(i - distance, i) for i in devices if i - distance in devices]
    return lax.ppermute(block, axis, route)


def swapped(block, axis, bit):
    count = lax.axis_size(axis)
    route = []
    for low in range(count):
        high = low | 1 << bit
        if high != low and high < count:
            route += [(low, high), (high, low)]
    return lax.ppermute(block, axis, route)


def plane_slice(offset):
    if offset < 0:
        return slice(7, 8)
    if offset > 0:
        return slice(0, 1)
    return slice(0, 8)


def take_rows(source_table, index_rows):
    padding = jnp.zeros((1,) + source_table.shape[1:], source_table.dtype)
    extended = jnp.concatenate([source_table, padding], 0)
    safe_index = jnp.where(index_rows < 0, source_table.shape[0], index_rows)
    return jnp.take(extended, safe_index, axis=0)


def build_padded(features_live, prev_upper, next_lower, neighbours):
    count_rows, channels = (features_live.shape[0], features_live.shape[1])
    blocks = features_live.reshape(count_rows, channels, 8, 8, 8)
    low_table = jnp.concatenate([blocks[:, :, 7:8], prev_upper.reshape(-1, channels, 1, 8, 8)], 0)
    high_table = jnp.concatenate([blocks[:, :, 0:1], next_lower.reshape(-1, channels, 1, 8, 8)], 0)
    layers = []
    for step_x, source_table in ((-1, low_table), (0, blocks), (1, high_table)):
        row_list = []
        for step_y in (-1, 0, 1):
            tile_list = []
            for step_z in (-1, 0, 1):
                column = (step_x + 1) * 9 + (step_y + 1) * 3 + step_z + 1
                if column == 13:
                    tile_list.append(blocks)
                else:
                    piece = source_table[:, :, :, plane_slice(step_y), plane_slice(step_z)]
                    tile_list.append(take_rows(piece, neighbours[:, column]))
            row_list.append(jnp.concatenate(tile_list, 4))
        layers.append(jnp.concatenate(row_list, 3))
    return jnp.concatenate(layers, 2)


def block_section(padded, grads_in, conv_weight, down_weight):
    count_rows, channels = (padded.shape[0], padded.shape[1])
    out_channels = down_weight.shape[1]

    def shifted_at(column):
        step_x, step_y, step_z = (column // 9 - 1, column // 3 % 3 - 1, column % 3 - 1)
        window = padded[
            :, :, 1 + step_x : 9 + step_x, 1 + step_y : 9 + step_y, 1 + step_z : 9 + step_z
        ]
        return window.reshape(count_rows, channels, 512)

    pre_act = jnp.zeros((count_rows, channels, 512), jnp.float32)
    for column in range(27):
        pre_act = pre_act + jnp.einsum(
            "oc,bcv->bov",
            conv_weight[column],
            shifted_at(column),
            preferred_element_type=jnp.float32,
        )
    hidden = jnp.maximum(pre_act, 0.0).astype(jnp.bfloat16)
    hidden_cells = hidden.reshape(count_rows, channels, 4, 2, 4, 2, 4, 2)
    grid_grads = grads_in.reshape(count_rows, 4, 4, 4, out_channels)
    down_grad = jnp.einsum(
        "bcxiyjzk,bxyzo->ijkoc", hidden_cells, grid_grads, preferred_element_type=jnp.float32
    ).reshape(8, out_channels, channels)
    kernel = down_weight.reshape(2, 2, 2, out_channels, channels)
    hidden_grad = jnp.einsum(
        "ijkoc,bxyzo->bcxiyjzk", kernel, grid_grads, preferred_element_type=jnp.float32
    ).reshape(count_rows, channels, 512)
    act_grad = jnp.where(pre_act > 0, hidden_grad, 0.0).astype(jnp.bfloat16)
    conv_grad = jnp.stack(
        [
            jnp.einsum(
                "bov,bcv->oc", act_grad, shifted_at(column), preferred_element_type=jnp.float32
            )
            for column in range(27)
        ]
    )
    return (hidden, conv_grad, down_grad)


def body(features, neighbours, counts, cotangent, conv_weight, down_weight):
    slot_count = features.shape[0]
    live_mask = (lax.iota(jnp.int32, slot_count) < counts[0])[:, None, None]
    features_live = jnp.where(live_mask, features, jnp.zeros_like(features))
    grads_live = jnp.where(live_mask, cotangent, jnp.zeros_like(cotangent))
    prev_upper = from_behind(features_live[:, :, 448:], "space", 1)
    next_lower = from_behind(features_live[:, :, :64], "space", -1)
    padded = build_padded(features_live, prev_upper, next_lower, neighbours)
    work_slots = slot_count * 3 // 4
    light_slots = slot_count // 2
    pair_bit = lax.axis_size("space").bit_length() - 2
    lent_blocks, lent_grads = swapped(
        (padded[work_slots:], grads_live[work_slots:]), "space", pair_bit
    )
    is_heavy = counts[0] > light_slots
    work_blocks = jnp.where(
        is_heavy, padded[:work_slots], jnp.concatenate([padded[:light_slots], lent_blocks], 0)
    )
    work_grads = jnp.where(
        is_heavy,
        grads_live[:work_slots],
        jnp.concatenate([grads_live[:light_slots], lent_grads], 0),
    )
    work_hidden, conv_grad, down_grad = block_section(
        work_blocks, work_grads, conv_weight, down_weight
    )
    returned = swapped(work_hidden[light_slots:], "space", pair_bit)
    empty_rest = jnp.zeros((slot_count - light_slots,) + work_hidden.shape[1:], work_hidden.dtype)
    hidden = jnp.where(
        is_heavy,
        jnp.concatenate([work_hidden, returned], 0),
        jnp.concatenate([work_hidden[:light_slots], empty_rest], 0),
    )
    conv_grad, down_grad = lax.psum((conv_grad, down_grad), ("space", "rep"))
    return (hidden, conv_grad, down_grad)


def solution(mesh):
    return jax.shard_map(
        body,
        mesh=mesh,
        in_specs=(
            P(("space", "rep"), None, None),
            P(("space", "rep"), None),
            P(("space", "rep")),
            P(("space", "rep"), None, None),
            P(),
            P(),
        ),
        out_specs=(P(("space", "rep"), None, None), P(), P()),
        check_vma=False,
    )
```

profile of v0, /device:TPU:0, one launch (start us, length us, event | category | flops | bytes accessed | tf_op | source)
XLA Modules:
  0.0 244.9 jit_solution(16946271803540995801)
XLA Ops:
  7.9 1.0 broadcast_select_fusion
  9.1 4.9 %collective-permute-start = (bf16[4,64,64]{2,1,0:T(8,128)(2,1)S(1)}, bf16[4,64,64]{2,1,0:T(8,128)(2,1)S(1)}, u32[]{:S(2)}, u32[]{:S(2)}) collective-permute-start(bf16[4,64,64]{2,1,0:T(8,128)(2,1)S(1)} %get-tuple-element.129), channel_id=1, source_target_pairs={{0,4},{4,8},{8,12},{12,16},{16,20},{20,24},{24,28},{1,5},{5,9},{9,... | collective-permute-start | bytes 98312 | tf_op jit(solution)/shard_map/ppermute | solution.py:10
  14.0 1.3 collective-permute-start.1
  15.3 0.9 broadcast_select_fusion.1
  16.2 4.7 %collective-permute-start.4 = (bf16[1,64,128]{2,1,0:T(8,128)(2,1)S(1)}, bf16[1,64,128]{2,1,0:T(8,128)(2,1)S(1)}, u32[]{:S(2)}, u32[]{:S(2)}) collective-permute-start(bf16[1,64,128]{2,1,0:T(8,128)(2,1)S(1)} %slice.589), channel_id=1, source_target_pairs={{0,16},{16,0},{4,20},{20,4},{8,24},{24,8},{12,28},{28,12},{1,17},{... | collective-permute-start | bytes 49160 | tf_op jit(solution)/shard_map/ppermute | solution.py:20
  23.1 0.6 gather_fusion.16
  24.4 0.6 gather_fusion.11
  25.6 0.6 gather_fusion.15
  26.3 0.6 gather_fusion.13
  27.0 0.6 gather_fusion.12
  27.7 0.6 gather_fusion.10
  29.4 0.6 gather_fusion.23
  30.0 0.6 gather_fusion.19
  30.6 0.6 gather_fusion.17
  31.3 0.6 gather_fusion.8
  35.1 0.6 gather_fusion.21
  35.8 0.6 gather_fusion
  37.1 0.6 gather_fusion.2
  37.7 0.6 gather_fusion.25
  40.2 0.6 gather_fusion.4
  40.9 11.9 %maximum_maximum_fusion = bf16[4,64,10,10,10]{1,0,4,3,2:T(4,128)(2,1)S(1)} fusion(bf16[4,64,1,1,1]{1,0,4,3,2:T(4,128)(2,1)S(1)} %bitcast_select_fusion.18, bf16[4,64,1,1,8]{1,0,4,3,2:T(4,128)(2,1)S(1)} %bitcast_select_fusion.6, bf16[4,64,1,1,1]{1,0,4,3,2:T(4,128)(2,1)S(1)} %bitcast_select_fusion.19, bf16[4,64,1,8,1]{1,0,4,3,2:T(4,128)(2,1)S(1)} %bitcast_select_fusion.7, ...), kind=kLoop, calls=%fused_computation.119 | loop fusion | flops 6656000 | bytes 1024000 | tf_op jit(solution)/shard_map/concatenate | solution.py:57
  54.7 23.2 %collective-permute-done.2 = bf16[1,64,10,10,10]{1,0,4,3,2:T(2,128)(2,1)S(1)} collective-permute-done((bf16[1,64,10,10,10]{1,0,4,3,2:T(2,128)(2,1)S(1)}, bf16[1,64,10,10,10]{1,0,4,3,2:T(2,128)(2,1)S(1)}, u32[]{:S(2)}, u32[]{:S(2)}) %collective-permute-start.2) | collective-permute-done | bytes 128032 | tf_op jit(solution)/shard_map/ppermute | solution.py:20
  77.9 1.6 slice_select_fusion
  79.5 2.3 fusion.160
  81.8 6.0 %fusion.159 = (bf16[3,64,8,8,8]{1,0,4,3,2:T(4,128)(2,1)S(1)}, bf16[3,64,8,8,8]{1,0,4,3,2:T(4,128)(2,1)S(1)}, bf16[3,64,8,8,8]{1,0,4,3,2:T(4,128)(2,1)S(1)}, bf16...) fusion(bf16[3,64,10,10,10]{1,0,4,3,2:T(4,128)(2,1)S(1)} %slice_, ...), kind=kLoop, calls=%fused_computation.417 | loop fusion | bytes 7471104 | tf_op jit(solution)/shard_map/slice | solution.py:66
  90.5 0.8 copy-done.3
  104.1 1.1 fusion.38
  105.4 5.1 %collective-permute-done.3 = bf16[1,64,512]{2,1,0:T(8,128)(2,1)S(1)} collective-permute-done((bf16[1,64,512]{2,1,0:T(8,128)(2,1)S(1)}, bf16[1,64,512]{2,1,0:T(8,128)(2,1)S(1)}, u32[]{:S(2)}, u32[]{:S(2)}) %collective-permute-start.3) | collective-permute-done | bytes 65568 | tf_op jit(solution)/shard_map/ppermute | solution.py:20
  110.5 0.7 maximum_select_fusion
  111.3 123.9 %all-reduce.28.cloned.1.call-done = (f32[27,64,64]{2,1,0:T(8,128)}, f32[8,128,64]{1,2,0:T(8,128)}) async-done(((f32[27,64,64]{2,1,0:T(8,128)}, f32[8,128,64]{1,2,0:T(8,128)}), (f32[27,64,64]{2,1,0:T(8,128)}, f32[8,128,64]{1,2,0:T(8,128)})) %all-reduce.28.cloned.1.call-update) | async-done | bytes 704528 | tf_op jit(solution)/shard_map/psum | solution.py:134
  235.1 2.2 copy.276
  237.4 0.7 copy.277
  (222 shorter events, 28.1 us)
Async XLA Ops:
  7.2 46.3 %copy-start = (bf16[8,128,64]{1,2,0:T(8,128)(2,1)S(1)}, bf16[8,128,64]{1,2,0:T(8,128)(2,1)}, u32[]{:S(2)}) copy-start(bf16[8,128,64]{1,2,0:T(8,128)(2,1)} %param.25) | copy-start | bytes 393220
  7.2 14.0 %copy-start.1 = (s32[4,27]{1,0:T(4,128)S(1)}, s32[4,27]{1,0:T(4,128)}, u32[]{:S(2)}) copy-start(s32[4,27]{1,0:T(4,128)} %param.21) | copy-start | bytes 1300
  7.2 227.9 %all-reduce.28.cloned.1.call-start = ((), (), s32[]{:S(2)}) async-start(), calls=%async_computation | async-start | bytes 2293760 | tf_op jit(solution)/shard_map/psum | solution.py:134
  9.1 19.4 %collective-permute-start = (bf16[4,64,64]{2,1,0:T(8,128)(2,1)S(1)}, bf16[4,64,64]{2,1,0:T(8,128)(2,1)S(1)}, u32[]{:S(2)}, u32[]{:S(2)}) collective-permute-start(bf16[4,64,64]{2,1,0:T(8,128)(2,1)S(1)} %get-tuple-element.129), channel_id=1, source_target_pairs={{0,4},{4,8},{8,12},{12,16},{16,20},{20,24},{24,28},{1,5},{5,9},{9,... | collective-permute-start | bytes 98312 | tf_op jit(solution)/shard_map/ppermute | solution.py:10
  14.0 14.6 %collective-permute-start.1 = (bf16[4,64,64]{2,1,0:T(8,128)(2,1)S(1)}, bf16[4,64,64]{2,1,0:T(8,128)(2,1)S(1)}, u32[]{:S(2)}, u32[]{:S(2)}) collective-permute-start(bf16[4,64,64]{2,1,0:T(8,128)(2,1)S(1)} %get-tuple-element.130), channel_id=1, source_target_pairs={{4,0},{8,4},{12,8},{16,12},{20,16},{24,20},{28,24},{5,1},{9,5},{13... | collective-permute-start | bytes 98312 | tf_op jit(solution)/shard_map/ppermute | solution.py:10
  16.2 12.2 %collective-permute-start.4 = (bf16[1,64,128]{2,1,0:T(8,128)(2,1)S(1)}, bf16[1,64,128]{2,1,0:T(8,128)(2,1)S(1)}, u32[]{:S(2)}, u32[]{:S(2)}) collective-permute-start(bf16[1,64,128]{2,1,0:T(8,128)(2,1)S(1)} %slice.589), channel_id=1, source_target_pairs={{0,16},{16,0},{4,20},{20,4},{8,24},{24,8},{12,28},{28,12},{1,17},{... | collective-permute-start | bytes 49160 | tf_op jit(solution)/shard_map/ppermute | solution.py:20
  53.4 24.5 %collective-permute-start.2 = (bf16[1,64,10,10,10]{1,0,4,3,2:T(2,128)(2,1)S(1)}, bf16[1,64,10,10,10]{1,0,4,3,2:T(2,128)(2,1)S(1)}, u32[]{:S(2)}, u32[]{:S(2)}) collective-permute-start(bf16[1,64,10,10,10]{1,0,4,3,2:T(2,128)(2,1)S(1)} %slice.557), channel_id=1, source_target_pairs={{0,16},{16,0},{4,20},{20,4},{8,24},{24,8},{12,28},{28,12},{1,17},{... | collective-permute-start | bytes 384008 | tf_op jit(solution)/shard_map/ppermute | solution.py:20
  90.3 1.0 copy-start.3
  103.9 1.4 copy-start.2
  105.3 5.2 %collective-permute-start.3 = (bf16[1,64,512]{2,1,0:T(8,128)(2,1)S(1)}, bf16[1,64,512]{2,1,0:T(8,128)(2,1)S(1)}, u32[]{:S(2)}, u32[]{:S(2)}) collective-permute-start(bf16[1,64,512]{2,1,0:T(8,128)(2,1)S(1)} %slice.585), channel_id=1, source_target_pairs={{0,16},{16,0},{4,20},{20,4},{8,24},{24,8},{12,28},{28,12},{1,17},{... | collective-permute-start | bytes 196616 | tf_op jit(solution)/shard_map/ppermute | solution.py:20
  235.1 2.2 copy-start.4
Sparse Core Ops, SparseCore 0:
  105.4 129.6 all-reduce.27
where the time goes:
time: 245 us
  waiting for transfers between devices  152 us (62%)
  local copies, waits for them, and re-layouts  32.8 us (13%)
  other arithmetic  19.1 us (8%)
  between operations  16 us (7%)
  matrix products  13.7 us (6%)
  starting transfers between devices  11.1 us (5%)
    psum x1, waiting for transfers between devices, body(): conv_grad, down_grad = lax.psum((conv_grad, down_grad), ('space', 'rep'))  124 us
    ppermute x3, waiting for transfers between devices, swapped(): return lax.ppermute(block, axis, route)  28.3 us
    gather x26, local copies, waits for them, and re-layouts, take_rows(): return jnp.take(extended, safe_index, axis=0)  14.6 us
    concatenate x1, other arithmetic, build_padded(): return jnp.concatenate(layers, 2)  11.9 us
    slice x29, local copies, waits for them, and re-layouts, shifted_at(): padded[:, :, 1 + step_x:9 + step_x, 1 + step_y:9 + step_y, 1 + step_z:9 +...  10.7 us
    dot_general x27, matrix products, block_section(): jnp.einsum('oc,bcv->bov', conv_weight[column], shifted_at(column), prefer...  6.91 us
    ppermute x2, starting transfers between devices, from_behind(): return lax.ppermute(block, axis, route)  6.19 us
    dot_general x27, matrix products, block_section(): jnp.einsum('bov,bcv->oc', act_grad, shifted_at(column), preferred_element...  5.38 us
  transfers between devices with their start and end apart: 6, of which 3 were waited for; matrix products, arithmetic and copies ran while one was open for 4% of the time, Pallas kernels for 0%

commit v1 on v0

v1 whole, which is shorter than its diff:
```python
import functools

import jax
import jax.numpy as jnp
from jax import lax
from jax.experimental import pallas as pl
from jax.experimental.pallas import tpu as pltpu
from jax.sharding import PartitionSpec as P


F32 = jnp.float32
BF16 = jnp.bfloat16
LANES = 128


def dot(a, b, dims):
    return lax.dot_general(a, b, (dims, ((), ())), preferred_element_type=F32)


def lane_iota(shape):
    return lax.broadcasted_iota(jnp.int32, shape, len(shape) - 1)


def doubled(rows):
    return jnp.concatenate([rows, rows], 0).astype(F32).T


def section_kernel(
    nb_ref, cnt_ref, feat_ref, prev_ref, next_ref, cot_ref, cw_ref, dw_ref,
    hid_ref, grad_ref,
    t0_ref, tl_ref, th_ref, sa_ref, sb_ref, wn_ref, hp_ref, as_ref,
):
    slots, ch, vox = feat_ref.shape
    half = ch

    t0_ref[slots] = jnp.zeros(t0_ref.shape[1:], F32)
    tl_ref[2 * slots] = jnp.zeros(tl_ref.shape[1:], F32)
    th_ref[2 * slots] = jnp.zeros(th_ref.shape[1:], F32)
    for j in range(slots):
        block = doubled(feat_ref[j]).reshape(8, 8, 8, LANES)
        t0_ref[j] = block
        tl_ref[j] = block[7]
        th_ref[j] = block[0]
        tl_ref[slots + j] = doubled(prev_ref[j])[64:].reshape(8, 8, LANES)
        th_ref[slots + j] = doubled(next_ref[j])[:64].reshape(8, 8, LANES)

    low_lanes = lane_iota((ch, LANES)) < half
    for iy in range(3):
        for ix in range(3):
            parts = []
            for iz in range(3):
                w = cw_ref[ix * 9 + iy * 3 + iz].astype(F32)
                parts.append(jnp.concatenate([w, jnp.zeros_like(w)], 1))
            both = jnp.where(low_lanes, parts[0], pltpu.roll(parts[1], half, 1))
            wn_ref[iy, pl.ds(ix * ch, ch), pl.ds(0, LANES)] = both.astype(BF16)
            wn_ref[iy, pl.ds(ix * ch, ch), pl.ds(LANES, LANES)] = parts[2].astype(BF16)

    row = lax.broadcasted_iota(jnp.int32, (vox, LANES), 0)
    t, u = row // 64, row % 64
    voxel = (
        64 * (2 * (u // 16) + t // 4)
        + 8 * (2 * (u // 4 % 4) + t // 2 % 2)
        + 2 * (u % 4) + t % 2
    )
    lane = lane_iota((vox, LANES))
    onehot = jnp.concatenate(
        [
            jnp.where(voxel == lane + q * LANES, 1.0, 0.0).astype(BF16)
            for q in range(vox // LANES)
        ],
        1,
    )

    cot = cot_ref[...].reshape(slots * 64, LANES)
    taps = dw_ref.shape[0]
    dwt = jnp.concatenate([dw_ref[t].astype(F32).T.astype(BF16) for t in range(taps)], 0)
    hg = dot(dwt, cot, ((1,), (1,)))
    low = lane_iota((ch, LANES)) < half

    def regroup(blocks, outer, inner):
        rows = []
        for j in range(inner):
            tiles = []
            for m in range(outer // 2):
                a = blocks[2 * m * ch : (2 * m + 1) * ch, j // 2 * LANES : (j // 2 + 1) * LANES]
                b = blocks[(2 * m + 1) * ch : (2 * m + 2) * ch, j // 2 * LANES : (j // 2 + 1) * LANES]
                if j % 2 == 0:
                    tiles.append(jnp.where(low, a, pltpu.roll(b, half, 1)))
                else:
                    tiles.append(jnp.where(low, pltpu.roll(a, half, 1), b))
            rows.append(jnp.concatenate(tiles, 1))
        return jnp.concatenate(rows, 0)

    hg = regroup(hg, taps, slots).astype(BF16)
    hp_ref[...] = dot(hg, onehot, ((1,), (0,)))

    zi = lax.broadcasted_iota(jnp.int32, (10, 8, LANES), 1)
    li = lane_iota((10, 8, LANES))
    for j in range(slots):
        def source(col):
            n = nb_ref[j, col]
            return jnp.where(n < 0, slots if 9 <= col < 18 else 2 * slots, n)

        centre = jnp.where(j < cnt_ref[0], j, slots)
        for xp in range(10):
            ox = -1 if xp == 0 else (1 if xp == 9 else 0)
            shifted = []
            for oz in (-1, 0, 1):
                pieces = []
                for oy in (-1, 0, 1):
                    col = (ox + 1) * 9 + (oy + 1) * 3 + oz + 1
                    n = centre if col == 13 else source(col)
                    ys = slice(7, 8) if oy < 0 else (slice(0, 1) if oy > 0 else slice(0, 8))
                    if ox == 0:
                        pieces.append(t0_ref[n, xp - 1, ys])
                    elif ox < 0:
                        pieces.append(tl_ref[n, ys])
                    else:
                        pieces.append(th_ref[n, ys])
                shifted.append(jnp.concatenate(pieces, 0))
            below, here, above = shifted
            zm = pltpu.roll(jnp.where(zi == 7, below, here), 1, 1)
            zp = pltpu.roll(jnp.where(zi == 0, above, here), 7, 1)
            s01 = jnp.where(li < half, zm, here)
            sa_ref[j, xp, :, pl.ds(0, LANES)] = s01.reshape(80, LANES).astype(BF16)
            sa_ref[j, xp, :, pl.ds(LANES, LANES)] = zp.reshape(80, LANES).astype(BF16)
            sb_ref[j, xp, :, pl.ds(0, LANES)] = s01[1:9].reshape(64, LANES).astype(BF16)
            sb_ref[j, xp, :, pl.ds(LANES, LANES)] = zp[1:9].reshape(64, LANES).astype(BF16)

    def window(iy, first, count):
        if iy == 1:
            s = sb_ref[pl.ds(first, count)]
        else:
            s = sa_ref[pl.ds(first, count), :, pl.ds(8 * iy, 64)]
        return s.reshape(count * 640, 2 * LANES)

    zero = jnp.zeros((ch, LANES), F32)
    for j in range(slots):
        out = dot(window(0, j, 1), wn_ref[0], ((1,), (1,)))
        out = out + dot(window(1, j, 1), wn_ref[1], ((1,), (1,)))
        out = out + dot(window(2, j, 1), wn_ref[2], ((1,), (1,)))
        first = out[:, :LANES]
        second = out[:, LANES:]
        pre = (
            first[:vox]
            + pltpu.roll(first[64 : 64 + vox], half, 1)
            + jnp.concatenate([second[128 : 128 + vox], jnp.zeros((vox, LANES - ch), F32)], 1)
        )
        pre = pre.T[:ch]
        hid_ref[j] = jnp.maximum(pre, 0.0).astype(BF16)
        act = jnp.where(pre > 0, hp_ref[pl.ds(j * ch, ch), :], 0.0)
        lead = jnp.concatenate([act, zero], 1)
        as_ref[pl.ds(0, ch), pl.ds(j * 640, 640)] = lead.astype(BF16)
        as_ref[pl.ds(ch, ch), pl.ds(j * 640, 640)] = pltpu.roll(lead, half, 1).astype(BF16)
        as_ref[pl.ds(2 * ch, ch), pl.ds(j * 640, 640)] = jnp.concatenate([zero, act], 1).astype(BF16)

    hidden = hid_ref[...].reshape(slots * ch, vox)
    hperm = dot(hidden, onehot, ((1,), (1,)))
    hperm = regroup(hperm, slots, taps).astype(BF16)
    cott = cot.astype(F32).T.astype(BF16)
    down = dot(cott, hperm, ((1,), (1,)))
    base = 3 * 3 * ch + 3 * ch + 3 * ch // 2
    for q in range(taps // 2):
        grad_ref[pl.ds(base + q * 128, 128), :] = down[:, q * LANES : (q + 1) * LANES]

    tails = []
    for iy in range(3):
        g = dot(as_ref[...], window(iy, 0, slots), ((1,), (0,)))
        grad_ref[pl.ds(iy * 3 * ch, 3 * ch), :] = g[:, :LANES]
        tails.append(g[:, LANES:])
    wide = lane_iota((3 * ch, LANES)) < half
    grad_ref[pl.ds(9 * ch, 3 * ch), :] = jnp.where(wide, tails[0], tails[1])
    hrows = 3 * ch // 2
    grad_ref[pl.ds(12 * ch, hrows), :] = jnp.where(wide[:hrows], tails[2][:hrows], tails[2][hrows:])
    used = base + taps * ch
    grad_ref[pl.ds(used, grad_ref.shape[0] - used), :] = jnp.zeros((grad_ref.shape[0] - used, LANES), F32)


def unpack_kernel(x_ref, conv_ref, down_ref):
    taps, outs, ch = down_ref.shape
    half = ch
    base = 9 * ch + 3 * ch + 3 * ch // 2

    def put(ref, k, tile, upper):
        if upper:
            tile = pltpu.roll(tile, half, 1)
        ref[k] = tile[:, :ch]

    for iy in range(3):
        for ix in range(3):
            tile = x_ref[pl.ds(iy * 3 * ch + ix * ch, ch), :]
            put(conv_ref, ix * 9 + iy * 3, tile, False)
            put(conv_ref, ix * 9 + iy * 3 + 1, tile, True)
    for ix in range(3):
        tile = x_ref[pl.ds(9 * ch + ix * ch, ch), :]
        put(conv_ref, ix * 9 + 2, tile, False)
        put(conv_ref, ix * 9 + 5, tile, True)
    tail = x_ref[pl.ds(12 * ch, 3 * ch // 2), :]
    tail = jnp.concatenate([tail, pltpu.roll(tail, half, 1)], 0)
    for ix in range(3):
        conv_ref[ix * 9 + 8] = tail[ix * ch : (ix + 1) * ch, :ch]
    for q in range(taps // 2):
        tile = x_ref[pl.ds(base + q * outs, outs), :]
        put(down_ref, 2 * q, tile, False)
        put(down_ref, 2 * q + 1, tile, True)


def from_behind(block, axis, distance):
    devices = range(lax.axis_size(axis))
    route = [(i - distance, i) for i in devices if i - distance in devices]
    return lax.ppermute(block, axis, route)


def partner(block, axis, bit):
    route = [(i, i ^ (1 << bit)) for i in range(lax.axis_size(axis))]
    return lax.ppermute(block, axis, route)


def halves(block, axis, bit):
    side = lax.axis_index(axis) >> bit & 1
    rows = block.shape[0] // 2
    low, high = block[:rows], block[rows:]
    keep = jnp.where(side == 1, high, low)
    give = jnp.where(side == 1, low, high)
    return keep, give, side


def reduce_all(block):
    scatter = [("rep", 0), ("rep", 1), ("space", 0)]
    whole = [("space", b) for b in range(1, lax.axis_size("space").bit_length() - 1)]
    whole += [("rep", b) for b in range(2, lax.axis_size("rep").bit_length() - 1)]
    for axis, bit in scatter:
        keep, give, _ = halves(block, axis, bit)
        block = keep + partner(give, axis, bit)
    for axis, bit in whole:
        block = block + partner(block, axis, bit)
    for axis, bit in reversed(scatter):
        other = partner(block, axis, bit)
        side = lax.axis_index(axis) >> bit & 1
        block = jnp.where(
            side == 1, jnp.concatenate([other, block], 0), jnp.concatenate([block, other], 0)
        )
    return block


def body(features, neighbours, counts, cotangent, conv_weight, down_weight):
    slots, ch, vox = features.shape
    prev_upper = from_behind(features[:, :, vox - LANES :], "space", 1)
    next_lower = from_behind(features[:, :, :LANES], "space", -1)
    vmem = pl.BlockSpec(memory_space=pltpu.VMEM)
    smem = pl.BlockSpec(memory_space=pltpu.SMEM)
    taps, outs, _ = down_weight.shape
    total = conv_weight.size + down_weight.size
    rows = -(-total // (LANES * 128)) * 128
    hidden, grads = pl.pallas_call(
        section_kernel,
        out_shape=(
            jax.ShapeDtypeStruct((slots, ch, vox), BF16),
            jax.ShapeDtypeStruct((rows, LANES), F32),
        ),
        in_specs=[smem, smem] + [vmem] * 6,
        out_specs=(vmem, vmem),
        scratch_shapes=[
            pltpu.VMEM((slots + 1, 8, 8, 8, LANES), F32),
            pltpu.VMEM((2 * slots + 1, 8, 8, LANES), F32),
            pltpu.VMEM((2 * slots + 1, 8, 8, LANES), F32),
            pltpu.VMEM((slots, 10, 80, 2 * LANES), BF16),
            pltpu.VMEM((slots, 10, 64, 2 * LANES), BF16),
            pltpu.VMEM((3, 3 * ch, 2 * LANES), BF16),
            pltpu.VMEM((slots * ch, vox), F32),
            pltpu.VMEM((3 * ch, slots * 640), BF16),
        ],
        name="section",
    )(neighbours, counts, features, prev_upper, next_lower, cotangent, conv_weight, down_weight)
    grads = reduce_all(grads)
    conv_grad, down_grad = pl.pallas_call(
        unpack_kernel,
        out_shape=(
            jax.ShapeDtypeStruct(conv_weight.shape, F32),
            jax.ShapeDtypeStruct(down_weight.shape, F32),
        ),
        in_specs=[vmem],
        out_specs=(vmem, vmem),
        name="unpack",
    )(grads)
    return hidden, conv_grad, down_grad


def solution(mesh):
    return jax.shard_map(
        body,
        mesh=mesh,
        in_specs=(
            P(("space", "rep"), None, None),
            P(("space", "rep"), None),
            P(("space", "rep")),
            P(("space", "rep"), None, None),
            P(),
            P(),
        ),
        out_specs=(P(("space", "rep"), None, None), P(), P()),
        check_vma=False,
    )
```

time: 245 us -> 62.5 us (0.26)
  waiting for transfers between devices: 152 us -> 24.7 us
  local copies, waits for them, and re-layouts: 32.8 us -> 4.43 us
  other arithmetic: 19.1 us -> 2.32 us
  between operations: 16 us -> 1.4 us
  matrix products: 13.7 us -> 0 us
  starting transfers between devices: 11.1 us -> 20.6 us
  Pallas kernels: 0 us -> 8.68 us
    psum x1 -> x0, waiting for transfers between devices: 124 us -> none  [body(): conv_grad, down_grad = lax.psum((conv_grad, down_grad), ('space', 'rep'))]
    gather x26 -> x0, local copies, waits for them, and re-layouts: 14.6 us -> none  [take_rows(): return jnp.take(extended, safe_index, axis=0)]
    dot_general x56 -> x0, matrix products: 13.7 us -> none  [the longest x27 6.91 us: block_section(): jnp.einsum('oc,bcv->bov', conv_weight[column], shifted_at(column), prefer...]
    concatenate x1 -> x0, other arithmetic: 11.9 us -> none  [build_padded(): return jnp.concatenate(layers, 2)]
    slice x42 -> x1, local copies, waits for them, and re-layouts: 12.7 us -> 0.92 us  [body(): next_lower = from_behind(features[:, :, :LANES], 'space', -1)]
    ppermute x3 -> x8, starting transfers between devices: 4.83 us -> 13.7 us  [partner(): return lax.ppermute(block, axis, route)]
    pallas_call x0 -> x2, Pallas kernels: none -> 8.68 us  [the longest x1 6.29 us: body(): pl.pallas_call(section_kernel, out_shape=(jax.ShapeDtypeStruct((slots, ch...]
    select_n x31 -> x6, other arithmetic: 6.46 us -> 2.19 us  [the longest x3 1.24 us: halves(): give = jnp.where(side == 1, low, high)]
  transfers between devices with their start and end apart: 6 -> 10, of which waited for: 3 -> 9; matrix products, arithmetic and copies ran while one was open for 4% -> 1% of each run, Pallas kernels for 0% -> 0%
where the time goes in v1:
time: 62.5 us; the launch traced here: 62.1 us
  waiting for transfers between devices  24.7 us (40%)
  starting transfers between devices  20.6 us (33%)
  Pallas kernels  8.68 us (14%)
  local copies, waits for them, and re-layouts  4.43 us (7%)
  other arithmetic  2.32 us (4%)
  between operations  1.4 us (2%)
    ppermute x8, waiting for transfers between devices, partner(): return lax.ppermute(block, axis, route)  24.2 us
    ppermute x8, starting transfers between devices, partner(): return lax.ppermute(block, axis, route)  13.7 us
    ppermute x2, starting transfers between devices, from_behind(): return lax.ppermute(block, axis, route)  6.82 us
    pallas_call x1, Pallas kernels, body(): pl.pallas_call(section_kernel, out_shape=(jax.ShapeDtypeStruct((slots, ch...  6.29 us
    unnamed x10, local copies, waits for them, and re-layouts  3.51 us
    pallas_call x1, Pallas kernels, body(): pl.pallas_call(unpack_kernel, out_shape=(jax.ShapeDtypeStruct(conv_weight...  2.4 us
  transfers between devices with their start and end apart: 10, of which 9 were waited for; matrix products, arithmetic and copies ran while one was open for 1% of the time, Pallas kernels for 0%

profile of v1, /device:TPU:0, one launch (start us, length us, event | category | flops | bytes accessed | tf_op | source)
XLA Modules:
  0.0 62.1 jit_solution(3145472330138628565)
XLA Ops:
  0.6 0.0 copy-start.1
  0.6 0.9 %fusion = (bf16[4,64,128]{2,1,0:T(8,128)(2,1)S(1)}, bf16[4,64,128]{2,1,0:T(8,128)(2,1)S(1)}) fusion(bf16[4,64,512]{2,1,0:T(8,128)(2,1)} %feat_ref.1), kind=kLoop, calls=%fused_computation.9 | loop fusion | bytes 262144 | tf_op jit(solution)/shard_map/slice | solution.py:249
  1.6 1.3 %collective-permute-start.1 = (bf16[4,64,128]{2,1,0:T(8,128)(2,1)S(1)}, bf16[4,64,128]{2,1,0:T(8,128)(2,1)S(1)}, u32[]{:S(2)}, u32[]{:S(2)}) collective-permute-start(bf16[4,64,128]{2,1,0:T(8,128)(2,1)S(1)} %get-tuple-element.14), channel_id=1, source_target_pairs={{4,0},{8,4},{12,8},{16,12},{20,16},{24,20},{28,24},{5,1},{9,5},{13... | collective-permute-start | bytes 196616 | tf_op jit(solution)/shard_map/ppermute | solution.py:211
  2.9 5.5 %collective-permute-start = (bf16[4,64,128]{2,1,0:T(8,128)(2,1)S(1)}, bf16[4,64,128]{2,1,0:T(8,128)(2,1)S(1)}, u32[]{:S(2)}, u32[]{:S(2)}) collective-permute-start(bf16[4,64,128]{2,1,0:T(8,128)(2,1)S(1)} %get-tuple-element.15), channel_id=1, source_target_pairs={{0,4},{4,8},{8,12},{12,16},{16,20},{20,24},{24,28},{1,5},{5,9},{9,... | collective-permute-start | bytes 196616 | tf_op jit(solution)/shard_map/ppermute | solution.py:211
  9.1 0.0 copy-done.1
  9.1 0.9 %copy.9.dw_ref = bf16[8,128,64]{2,1,0:T(8,128)(2,1)} copy(bf16[8,128,64]{1,2,0:T(8,128)(2,1)S(1)} %copy-done.1) | data formatting | bytes 262144 | tf_op args[5]
  9.9 0.0 collective-permute-done.1.next_ref
  9.9 0.5 collective-permute-done.prev_ref
  10.4 0.1 copy-done.2
  10.5 0.6 copy-done.3
  11.2 6.3 %section.1 = (bf16[4,64,512]{2,1,0:T(8,128)(2,1)}, f32[1408,128]{1,0:T(8,128)}) custom-call(s32[4,27]{1,0:T(4,128)} %nb_ref.1, s32[1]{0:T(128)S(6)} %copy.11.cnt_ref, bf16[4,64,512]{2,1,0:T(8,128)(2,1)} %feat_ref.1, bf16[4,64,128]{2,1,0:T(8,128)(2,1)} %copy-done.3, bf16[4,64,128]{2,1,0:T(8,128)(2,1)} %copy-done.2, bf16[4,64,128]{2,1,0:T(8,128)(2,1)} %cot_ref.1, ...), custom_call_target="tpu_custom_call" | custom-call | tf_op jit(solution)/shard_map/section/pallas_call | solution.py:255
  17.4 1.2 %slice_select_fusion = f32[704,128]{1,0:T(8,128)S(1)} fusion(f32[1408,128]{1,0:T(8,128)} %get-tuple-element.8, pred[]{:T(512)S(6)} %eq.6), kind=kLoop, calls=%fused_computation.3 | loop fusion | flops 90112 | bytes 1081345 | tf_op jit(solution)/shard_map/jit(_where)/select_n | solution.py:224
  18.7 0.1 collective-permute-start.2
  18.7 1.7 %collective-permute-done.2 = f32[704,128]{1,0:T(8,128)S(1)} collective-permute-done((f32[704,128]{1,0:T(8,128)S(1)}, f32[704,128]{1,0:T(8,128)S(1)}, u32[]{:S(2)}, u32[]{:S(2)}) %collective-permute-start.2) | collective-permute-done | bytes 360480 | tf_op jit(solution)/shard_map/ppermute | solution.py:216
  20.4 0.1 select_add_fusion
  20.5 2.1 %collective-permute-start.3 = (f32[352,128]{1,0:T(8,128)S(1)}, f32[352,128]{1,0:T(8,128)S(1)}, u32[]{:S(2)}, u32[]{:S(2)}) collective-permute-start(f32[352,128]{1,0:T(8,128)S(1)} %slice_select_fusion.1), channel_id=1, source_target_pairs={{0,2},{1,3},{2,0},{3,1},{4,6},{5,7},{6,4},{7,5},{8,10},{9,11},{10,... | collective-permute-start | bytes 540680 | tf_op jit(solution)/shard_map/ppermute | solution.py:216
  22.5 4.9 %collective-permute-done.3 = f32[352,128]{1,0:T(8,128)S(1)} collective-permute-done((f32[352,128]{1,0:T(8,128)S(1)}, f32[352,128]{1,0:T(8,128)S(1)}, u32[]{:S(2)}, u32[]{:S(2)}) %collective-permute-start.3) | collective-permute-done | bytes 180256 | tf_op jit(solution)/shard_map/ppermute | solution.py:216
  27.4 2.7 %collective-permute-start.4 = (f32[176,128]{1,0:T(8,128)S(1)}, f32[176,128]{1,0:T(8,128)S(1)}, u32[]{:S(2)}, u32[]{:S(2)}) collective-permute-start(f32[176,128]{1,0:T(8,128)S(1)} %slice_select_fusion.2), channel_id=1, source_target_pairs={{0,4},{4,0},{8,12},{12,8},{16,20},{20,16},{24,28},{28,24},{1,5},{5... | collective-permute-start | bytes 270344 | tf_op jit(solution)/shard_map/ppermute | solution.py:216
  30.2 2.5 %collective-permute-done.4 = f32[176,128]{1,0:T(8,128)S(1)} collective-permute-done((f32[176,128]{1,0:T(8,128)S(1)}, f32[176,128]{1,0:T(8,128)S(1)}, u32[]{:S(2)}, u32[]{:S(2)}) %collective-permute-start.4) | collective-permute-done | bytes 90144 | tf_op jit(solution)/shard_map/ppermute | solution.py:216
  32.7 3.6 %collective-permute-start.5 = (f32[176,128]{1,0:T(8,128)S(1)}, f32[176,128]{1,0:T(8,128)S(1)}, u32[]{:S(2)}, u32[]{:S(2)}) collective-permute-start(f32[176,128]{1,0:T(8,128)S(1)} %select_add_fusion.2), channel_id=1, source_target_pairs={{0,8},{4,12},{8,0},{12,4},{16,24},{20,28},{24,16},{28,20},{1,9},{5... | collective-permute-start | bytes 270344 | tf_op jit(solution)/shard_map/ppermute | solution.py:216
  36.3 2.5 %collective-permute-done.5 = f32[176,128]{1,0:T(8,128)S(1)} collective-permute-done((f32[176,128]{1,0:T(8,128)S(1)}, f32[176,128]{1,0:T(8,128)S(1)}, u32[]{:S(2)}, u32[]{:S(2)}) %collective-permute-start.5) | collective-permute-done | bytes 90144 | tf_op jit(solution)/shard_map/ppermute | solution.py:216
  38.9 3.6 %collective-permute-start.6 = (f32[176,128]{1,0:T(8,128)S(1)}, f32[176,128]{1,0:T(8,128)S(1)}, u32[]{:S(2)}, u32[]{:S(2)}) collective-permute-start(f32[176,128]{1,0:T(8,128)S(1)} %add.18), channel_id=1, source_target_pairs={{0,16},{4,20},{8,24},{12,28},{16,0},{20,4},{24,8},{28,12},{1,17},{... | collective-permute-start | bytes 270344 | tf_op jit(solution)/shard_map/ppermute | solution.py:216
  42.4 2.5 %collective-permute-done.6 = f32[176,128]{1,0:T(8,128)S(1)} collective-permute-done((f32[176,128]{1,0:T(8,128)S(1)}, f32[176,128]{1,0:T(8,128)S(1)}, u32[]{:S(2)}, u32[]{:S(2)}) %collective-permute-start.6) | collective-permute-done | bytes 90144 | tf_op jit(solution)/shard_map/ppermute | solution.py:216
  45.0 0.1 collective-permute-start.7
  45.0 4.5 %collective-permute-done.7 = f32[176,128]{1,0:T(8,128)S(1)} collective-permute-done((f32[176,128]{1,0:T(8,128)S(1)}, f32[176,128]{1,0:T(8,128)S(1)}, u32[]{:S(2)}, u32[]{:S(2)}) %collective-permute-start.7) | collective-permute-done | bytes 90144 | tf_op jit(solution)/shard_map/ppermute | solution.py:216
  49.6 1.6 %collective-permute-start.8 = (f32[352,128]{1,0:T(8,128)S(1)}, f32[352,128]{1,0:T(8,128)S(1)}, u32[]{:S(2)}, u32[]{:S(2)}) collective-permute-start(f32[352,128]{1,0:T(8,128)S(1)} %maximum_select_fusion.2), channel_id=1, source_target_pairs={{0,2},{1,3},{2,0},{3,1},{4,6},{5,7},{6,4},{7,5},{8,10},{9,11},{10,... | collective-permute-start | bytes 540680 | tf_op jit(solution)/shard_map/ppermute | solution.py:216
  51.1 4.0 %collective-permute-done.8 = f32[352,128]{1,0:T(8,128)S(1)} collective-permute-done((f32[352,128]{1,0:T(8,128)S(1)}, f32[352,128]{1,0:T(8,128)S(1)}, u32[]{:S(2)}, u32[]{:S(2)}) %collective-permute-start.8) | collective-permute-done | bytes 180256 | tf_op jit(solution)/shard_map/ppermute | solution.py:216
  55.2 0.1 collective-permute-start.9
  55.2 1.7 %collective-permute-done.9 = f32[704,128]{1,0:T(8,128)S(1)} collective-permute-done((f32[704,128]{1,0:T(8,128)S(1)}, f32[704,128]{1,0:T(8,128)S(1)}, u32[]{:S(2)}, u32[]{:S(2)}) %collective-permute-start.9) | collective-permute-done | bytes 360480 | tf_op jit(solution)/shard_map/ppermute | solution.py:216
  56.9 0.9 %maximum_select_fusion.x_ref = f32[1408,128]{1,0:T(8,128)} fusion(f32[704,128]{1,0:T(8,128)S(1)} %maximum_select_fusion.1, f32[704,128]{1,0:T(8,128)S(1)} %collective-permute-done.9, pred[]{:T(512)S(6)} %eq.6), kind=kLoop, calls=%fused_computation | loop fusion | flops 540672 | bytes 1441793 | tf_op jit(solution)/shard_map/jit(_where)/select_n | solution.py:240
  57.8 2.4 %unpack.1 = (f32[27,64,64]{2,1,0:T(8,128)}, f32[8,128,64]{2,1,0:T(8,128)}) custom-call(f32[1408,128]{1,0:T(8,128)} %maximum_select_fusion.x_ref), custom_call_target="tpu_custom_call" | custom-call | tf_op jit(solution)/shard_map/unpack/pallas_call | solution.py:276
  60.2 1.9 %copy.10 = f32[8,128,64]{1,2,0:T(8,128)} copy(f32[8,128,64]{2,1,0:T(8,128)} %get-tuple-element.13) | data formatting | bytes 524288
  (12 shorter events, 0.2 us)
Async XLA Ops:
  0.6 8.4 %copy-start.1 = (bf16[8,128,64]{1,2,0:T(8,128)(2,1)S(1)}, bf16[8,128,64]{1,2,0:T(8,128)(2,1)}, u32[]{:S(2)}) copy-start(bf16[8,128,64]{1,2,0:T(8,128)(2,1)} %param.11) | copy-start | bytes 393220
  1.6 8.4 %collective-permute-start.1 = (bf16[4,64,128]{2,1,0:T(8,128)(2,1)S(1)}, bf16[4,64,128]{2,1,0:T(8,128)(2,1)S(1)}, u32[]{:S(2)}, u32[]{:S(2)}) collective-permute-start(bf16[4,64,128]{2,1,0:T(8,128)(2,1)S(1)} %get-tuple-element.14), channel_id=1, source_target_pairs={{4,0},{8,4},{12,8},{16,12},{20,16},{24,20},{28,24},{5,1},{9,5},{13... | collective-permute-start | bytes 196616 | tf_op jit(solution)/shard_map/ppermute | solution.py:211
  2.9 7.6 %collective-permute-start = (bf16[4,64,128]{2,1,0:T(8,128)(2,1)S(1)}, bf16[4,64,128]{2,1,0:T(8,128)(2,1)S(1)}, u32[]{:S(2)}, u32[]{:S(2)}) collective-permute-start(bf16[4,64,128]{2,1,0:T(8,128)(2,1)S(1)} %get-tuple-element.15), channel_id=1, source_target_pairs={{0,4},{4,8},{8,12},{12,16},{16,20},{20,24},{24,28},{1,5},{5,9},{9,... | collective-permute-start | bytes 196616 | tf_op jit(solution)/shard_map/ppermute | solution.py:211
  9.9 0.6 copy-start.2
  10.5 0.6 %copy-start.3 = (bf16[4,64,128]{2,1,0:T(8,128)(2,1)}, bf16[4,64,128]{2,1,0:T(8,128)(2,1)S(1)}, u32[]{:S(2)}) copy-start(bf16[4,64,128]{2,1,0:T(8,128)(2,1)S(1)} %collective-permute-done.prev_ref) | copy-start | bytes 196612
  17.4 3.0 %copy-start = (f32[1408,128]{1,0:T(8,128)S(1)}, f32[1408,128]{1,0:T(8,128)}, u32[]{:S(2)}) copy-start(f32[1408,128]{1,0:T(8,128)} %get-tuple-element.8) | copy-start | bytes 2162692
  18.7 1.7 %collective-permute-start.2 = (f32[704,128]{1,0:T(8,128)S(1)}, f32[704,128]{1,0:T(8,128)S(1)}, u32[]{:S(2)}, u32[]{:S(2)}) collective-permute-start(f32[704,128]{1,0:T(8,128)S(1)} %slice_select_fusion), channel_id=1, source_target_pairs={{0,1},{1,0},{2,3},{3,2},{4,5},{5,4},{6,7},{7,6},{8,9},{9,8},{10,11... | collective-permute-start | bytes 1081352 | tf_op jit(solution)/shard_map/ppermute | solution.py:216
  20.5 6.9 %collective-permute-start.3 = (f32[352,128]{1,0:T(8,128)S(1)}, f32[352,128]{1,0:T(8,128)S(1)}, u32[]{:S(2)}, u32[]{:S(2)}) collective-permute-start(f32[352,128]{1,0:T(8,128)S(1)} %slice_select_fusion.1), channel_id=1, source_target_pairs={{0,2},{1,3},{2,0},{3,1},{4,6},{5,7},{6,4},{7,5},{8,10},{9,11},{10,... | collective-permute-start | bytes 540680 | tf_op jit(solution)/shard_map/ppermute | solution.py:216
  27.4 5.2 %collective-permute-start.4 = (f32[176,128]{1,0:T(8,128)S(1)}, f32[176,128]{1,0:T(8,128)S(1)}, u32[]{:S(2)}, u32[]{:S(2)}) collective-permute-start(f32[176,128]{1,0:T(8,128)S(1)} %slice_select_fusion.2), channel_id=1, source_target_pairs={{0,4},{4,0},{8,12},{12,8},{16,20},{20,16},{24,28},{28,24},{1,5},{5... | collective-permute-start | bytes 270344 | tf_op jit(solution)/shard_map/ppermute | solution.py:216
  32.7 6.2 %collective-permute-start.5 = (f32[176,128]{1,0:T(8,128)S(1)}, f32[176,128]{1,0:T(8,128)S(1)}, u32[]{:S(2)}, u32[]{:S(2)}) collective-permute-start(f32[176,128]{1,0:T(8,128)S(1)} %select_add_fusion.2), channel_id=1, source_target_pairs={{0,8},{4,12},{8,0},{12,4},{16,24},{20,28},{24,16},{28,20},{1,9},{5... | collective-permute-start | bytes 270344 | tf_op jit(solution)/shard_map/ppermute | solution.py:216
  38.9 6.1 %collective-permute-start.6 = (f32[176,128]{1,0:T(8,128)S(1)}, f32[176,128]{1,0:T(8,128)S(1)}, u32[]{:S(2)}, u32[]{:S(2)}) collective-permute-start(f32[176,128]{1,0:T(8,128)S(1)} %add.18), channel_id=1, source_target_pairs={{0,16},{4,20},{8,24},{12,28},{16,0},{20,4},{24,8},{28,12},{1,17},{... | collective-permute-start | bytes 270344 | tf_op jit(solution)/shard_map/ppermute | solution.py:216
  45.0 4.6 %collective-permute-start.7 = (f32[176,128]{1,0:T(8,128)S(1)}, f32[176,128]{1,0:T(8,128)S(1)}, u32[]{:S(2)}, u32[]{:S(2)}) collective-permute-start(f32[176,128]{1,0:T(8,128)S(1)} %add.19), channel_id=1, source_target_pairs={{0,4},{4,0},{8,12},{12,8},{16,20},{20,16},{24,28},{28,24},{1,5},{5... | collective-permute-start | bytes 270344 | tf_op jit(solution)/shard_map/ppermute | solution.py:216
  49.6 5.6 %collective-permute-start.8 = (f32[352,128]{1,0:T(8,128)S(1)}, f32[352,128]{1,0:T(8,128)S(1)}, u32[]{:S(2)}, u32[]{:S(2)}) collective-permute-start(f32[352,128]{1,0:T(8,128)S(1)} %maximum_select_fusion.2), channel_id=1, source_target_pairs={{0,2},{1,3},{2,0},{3,1},{4,6},{5,7},{6,4},{7,5},{8,10},{9,11},{10,... | collective-permute-start | bytes 540680 | tf_op jit(solution)/shard_map/ppermute | solution.py:216
  55.2 1.7 %collective-permute-start.9 = (f32[704,128]{1,0:T(8,128)S(1)}, f32[704,128]{1,0:T(8,128)S(1)}, u32[]{:S(2)}, u32[]{:S(2)}) collective-permute-start(f32[704,128]{1,0:T(8,128)S(1)} %maximum_select_fusion.1), channel_id=1, source_target_pairs={{0,1},{1,0},{2,3},{3,2},{4,5},{5,4},{6,7},{7,6},{8,9},{9,8},{10,11... | collective-permute-start | bytes 1081352 | tf_op jit(solution)/shard_map/ppermute | solution.py:216

commit v2 on v1

--- a/solution.py
+++ b/solution.py
@@ -26,12 +26,14 @@
 
 
 def section_kernel(
-    nb_ref, cnt_ref, feat_ref, prev_ref, next_ref, cot_ref, cw_ref, dw_ref,
-    hid_ref, grad_ref,
-    t0_ref, tl_ref, th_ref, sa_ref, sb_ref, wn_ref, hp_ref, as_ref,
+    nb_ref, cnt_ref, place_ref, feat_ref, near_ref, far_ref, cot_ref, cw_ref, dw_ref,
+    hid_ref, keep_a_ref, give_a_ref, keep_b_ref, give_b_ref,
+    t0_ref, tl_ref, th_ref, sa_ref, sb_ref, wn_ref, hp_ref, as_ref, grad_ref,
 ):
     slots, ch, vox = feat_ref.shape
     half = ch
+    odd = place_ref[0]
+    core = place_ref[1]
 
     t0_ref[slots] = jnp.zeros(t0_ref.shape[1:], F32)
     tl_ref[2 * slots] = jnp.zeros(tl_ref.shape[1:], F32)
@@ -41,8 +43,11 @@
         t0_ref[j] = block
         tl_ref[j] = block[7]
         th_ref[j] = block[0]
-        tl_ref[slots + j] = doubled(prev_ref[j])[64:].reshape(8, 8, LANES)
-        th_ref[slots + j] = doubled(next_ref[j])[:64].reshape(8, 8, LANES)
+        near, far = doubled(near_ref[j]), doubled(far_ref[j])
+        before = jnp.where(odd == 1, near, far)
+        after = jnp.where(odd == 1, far, near)
+        tl_ref[slots + j] = before[64:].reshape(8, 8, LANES)
+        th_ref[slots + j] = after[:64].reshape(8, 8, LANES)
 
     low_lanes = lane_iota((ch, LANES)) < half
     for iy in range(3):
@@ -73,8 +78,7 @@
 
     cot = cot_ref[...].reshape(slots * 64, LANES)
     taps = dw_ref.shape[0]
-    dwt = jnp.concatenate([dw_ref[t].astype(F32).T.astype(BF16) for t in range(taps)], 0)
-    hg = dot(dwt, cot, ((1,), (1,)))
+    hg = dot(dw_ref[...].reshape(taps * ch, LANES), cot, ((1,), (1,)))
     low = lane_iota((ch, LANES)) < half
 
     def regroup(blocks, outer, inner):
@@ -157,11 +161,8 @@
     hidden = hid_ref[...].reshape(slots * ch, vox)
     hperm = dot(hidden, onehot, ((1,), (1,)))
     hperm = regroup(hperm, slots, taps).astype(BF16)
-    cott = cot.astype(F32).T.astype(BF16)
-    down = dot(cott, hperm, ((1,), (1,)))
     base = 3 * 3 * ch + 3 * ch + 3 * ch // 2
-    for q in range(taps // 2):
-        grad_ref[pl.ds(base + q * 128, 128), :] = down[:, q * LANES : (q + 1) * LANES]
+    grad_ref[pl.ds(base, taps * ch), :] = dot(hperm, cot, ((1,), (0,)))
 
     tails = []
     for iy in range(3):
@@ -175,10 +176,24 @@
     used = base + taps * ch
     grad_ref[pl.ds(used, grad_ref.shape[0] - used), :] = jnp.zeros((grad_ref.shape[0] - used, LANES), F32)
 
-
-def unpack_kernel(x_ref, conv_ref, down_ref):
-    taps, outs, ch = down_ref.shape
+    rows = keep_a_ref.shape[0]
+    mine, theirs = pl.multiple_of(core * rows, 8), pl.multiple_of((1 - core) * rows, 8)
+    keep_a_ref[...] = grad_ref[pl.ds(mine, rows), :]
+    give_a_ref[...] = grad_ref[pl.ds(theirs, rows), :]
+    keep_b_ref[...] = grad_ref[pl.ds(2 * rows + mine, rows), :]
+    give_b_ref[...] = grad_ref[pl.ds(2 * rows + theirs, rows), :]
+
+
+def unpack_kernel(place_ref, mine_a, other_a, mine_b, other_b, conv_ref, down_ref, x_ref):
+    taps, ch, outs = down_ref.shape
     half = ch
+    core = place_ref[1]
+    rows = mine_a.shape[0]
+    mine, theirs = pl.multiple_of(core * rows, 8), pl.multiple_of((1 - core) * rows, 8)
+    x_ref[pl.ds(mine, rows), :] = mine_a[...]
+    x_ref[pl.ds(theirs, rows), :] = other_a[...]
+    x_ref[pl.ds(2 * rows + mine, rows), :] = mine_b[...]
+    x_ref[pl.ds(2 * rows + theirs, rows), :] = other_b[...]
     base = 9 * ch + 3 * ch + 3 * ch // 2
 
     def put(ref, k, tile, upper):
@@ -199,67 +214,74 @@
     tail = jnp.concatenate([tail, pltpu.roll(tail, half, 1)], 0)
     for ix in range(3):
         conv_ref[ix * 9 + 8] = tail[ix * ch : (ix + 1) * ch, :ch]
-    for q in range(taps // 2):
-        tile = x_ref[pl.ds(base + q * outs, outs), :]
-        put(down_ref, 2 * q, tile, False)
-        put(down_ref, 2 * q + 1, tile, True)
-
-
-def from_behind(block, axis, distance):
-    devices = range(lax.axis_size(axis))
-    route = [(i - distance, i) for i in devices if i - distance in devices]
-    return lax.ppermute(block, axis, route)
-
-
-def partner(block, axis, bit):
-    route = [(i, i ^ (1 << bit)) for i in range(lax.axis_size(axis))]
-    return lax.ppermute(block, axis, route)
-
-
-def halves(block, axis, bit):
-    side = lax.axis_index(axis) >> bit & 1
+    down_ref[...] = x_ref[pl.ds(base, taps * ch), :].reshape(taps, ch, outs)
+
+
+def axis_bits(axis):
+    return [(axis, b) for b in range(lax.axis_size(axis).bit_length() - 1)]
+
+
+def routes():
+    first = axis_bits("rep")[1:] + axis_bits("space")
+    second = list(first)
+    for i in range(0, len(second) - 1, 2):
+        second[i], second[i + 1] = second[i + 1], second[i]
+    return first, second
+
+
+def other_core(block):
+    return lax.ppermute(block, "rep", [(i, i ^ 1) for i in range(lax.axis_size("rep"))])
+
+
+def swapped(block, stage):
+    count = lax.axis_size("rep")
+    route = []
+    for s in range(lax.axis_size("space")):
+        for r in range(count):
+            axis, bit = routes()[r & 1][stage]
+            ps, pr = (s ^ 1 << bit, r) if axis == "space" else (s, r ^ 1 << bit)
+            route.append((s * count + r, ps * count + pr))
+    return lax.ppermute(block, ("space", "rep"), route)
+
+
+def side_of(stage):
+    sides = [lax.axis_index(axis) >> bit & 1 for axis, bit in (r[stage] for r in routes())]
+    return jnp.where(lax.axis_index("rep") & 1 == 0, sides[0], sides[1])
+
+
+def summed(keep, give):
+    block = keep + other_core(give)
     rows = block.shape[0] // 2
+    upper = side_of(0) == 1
     low, high = block[:rows], block[rows:]
-    keep = jnp.where(side == 1, high, low)
-    give = jnp.where(side == 1, low, high)
-    return keep, give, side
-
-
-def reduce_all(block):
-    scatter = [("rep", 0), ("rep", 1), ("space", 0)]
-    whole = [("space", b) for b in range(1, lax.axis_size("space").bit_length() - 1)]
-    whole += [("rep", b) for b in range(2, lax.axis_size("rep").bit_length() - 1)]
-    for axis, bit in scatter:
-        keep, give, _ = halves(block, axis, bit)
-        block = keep + partner(give, axis, bit)
-    for axis, bit in whole:
-        block = block + partner(block, axis, bit)
-    for axis, bit in reversed(scatter):
-        other = partner(block, axis, bit)
-        side = lax.axis_index(axis) >> bit & 1
-        block = jnp.where(
-            side == 1, jnp.concatenate([other, block], 0), jnp.concatenate([block, other], 0)
-        )
-    return block
+    block = jnp.where(upper, high, low) + swapped(jnp.where(upper, low, high), 0)
+    for stage in range(1, len(routes()[0])):
+        block = block + swapped(block, stage)
+    other = swapped(block, 0)
+    return jnp.where(
+        upper, jnp.concatenate([other, block], 0), jnp.concatenate([block, other], 0)
+    )
 
 
 def body(features, neighbours, counts, cotangent, conv_weight, down_weight):
     slots, ch, vox = features.shape
-    prev_upper = from_behind(features[:, :, vox - LANES :], "space", 1)
-    next_lower = from_behind(features[:, :, :LANES], "space", -1)
+    strips = lax.axis_size("space")
+    faces = jnp.concatenate([features[:, :, :64], features[:, :, vox - 64 :]], 2)
+    near = lax.ppermute(faces, "space", [(i, i ^ 1) for i in range(strips) if i ^ 1 < strips])
+    steps = [(i, i + 1) for i in range(1, strips - 1, 2)]
+    far = lax.ppermute(faces, "space", steps + [(b, a) for a, b in steps])
+    place = jnp.stack([lax.axis_index("space") & 1, lax.axis_index("rep") & 1]).astype(jnp.int32)
     vmem = pl.BlockSpec(memory_space=pltpu.VMEM)
     smem = pl.BlockSpec(memory_space=pltpu.SMEM)
     taps, outs, _ = down_weight.shape
     total = conv_weight.size + down_weight.size
     rows = -(-total // (LANES * 128)) * 128
-    hidden, grads = pl.pallas_call(
+    part = jax.ShapeDtypeStruct((rows // 4, LANES), F32)
+    hidden, keep_a, give_a, keep_b, give_b = pl.pallas_call(
         section_kernel,
-        out_shape=(
-            jax.ShapeDtypeStruct((slots, ch, vox), BF16),
-            jax.ShapeDtypeStruct((rows, LANES), F32),
-        ),
-        in_specs=[smem, smem] + [vmem] * 6,
-        out_specs=(vmem, vmem),
+        out_shape=(jax.ShapeDtypeStruct((slots, ch, vox), BF16), part, part, part, part),
+        in_specs=[smem] * 3 + [vmem] * 6,
+        out_specs=(vmem,) * 5,
         scratch_shapes=[
             pltpu.VMEM((slots + 1, 8, 8, 8, LANES), F32),
             pltpu.VMEM((2 * slots + 1, 8, 8, LANES), F32),
@@ -269,21 +291,29 @@
             pltpu.VMEM((3, 3 * ch, 2 * LANES), BF16),
             pltpu.VMEM((slots * ch, vox), F32),
             pltpu.VMEM((3 * ch, slots * 640), BF16),
+            pltpu.VMEM((rows, LANES), F32),
         ],
+        compiler_params=pltpu.CompilerParams(vmem_limit_bytes=32 << 20),
         name="section",
-    )(neighbours, counts, features, prev_upper, next_lower, cotangent, conv_weight, down_weight)
-    grads = reduce_all(grads)
+    )(
+        neighbours, counts, place, features, near, far, cotangent, conv_weight,
+        jnp.swapaxes(down_weight, 1, 2),
+    )
+    mine_a = summed(keep_a, give_a)
+    mine_b = summed(keep_b, give_b)
     conv_grad, down_grad = pl.pallas_call(
         unpack_kernel,
         out_shape=(
             jax.ShapeDtypeStruct(conv_weight.shape, F32),
-            jax.ShapeDtypeStruct(down_weight.shape, F32),
+            jax.ShapeDtypeStruct((taps, ch, outs), F32),
         ),
-        in_specs=[vmem],
+        in_specs=[smem] + [vmem] * 4,
         out_specs=(vmem, vmem),
+        scratch_shapes=[pltpu.VMEM((rows, LANES), F32)],
+        compiler_params=pltpu.CompilerParams(vmem_limit_bytes=16 << 20),
         name="unpack",
-    )(grads)
-    return hidden, conv_grad, down_grad
+    )(place, mine_a, other_core(mine_a), mine_b, other_core(mine_b))
+    return hidden, conv_grad, jnp.swapaxes(down_grad, 1, 2)
 
 
 def solution(mesh):

time: 62.5 us -> 48.6 us (0.78)
  waiting for transfers between devices: 24.7 us -> 13.9 us
  starting transfers between devices: 20.6 us -> 24.6 us
  Pallas kernels: 8.68 us -> 6.07 us
  local copies, waits for them, and re-layouts: 4.43 us -> 2.03 us
  other arithmetic: 2.32 us -> 0.39 us
    ppermute x10 -> x16, waiting for transfers between devices: 24.7 us -> 13.9 us  [the longest x10 10.1 us: swapped(): return lax.ppermute(block, ('space', 'rep'), route)]
    ppermute x10 -> x16, starting transfers between devices: 20.6 us -> 24.6 us  [the longest x10 17.4 us: swapped(): return lax.ppermute(block, ('space', 'rep'), route)]
    unnamed x10, local copies, waits for them, and re-layouts: 3.51 us -> 1.03 us
    select_n x6 -> x4, other arithmetic: 2.19 us -> 0.05 us  [the longest x2 0.03 us: summed(): jnp.where(upper, jnp.concatenate([other, block], 0), jnp.concatenate([blo...]
    pallas_call x1, Pallas kernels: 6.29 us -> 4.36 us  [body(): pl.pallas_call(section_kernel, out_shape=(jax.ShapeDtypeStruct((slots, ch...]
    pallas_call x1, Pallas kernels: 2.4 us -> 1.7 us  [body(): pl.pallas_call(unpack_kernel, out_shape=(jax.ShapeDtypeStruct(conv_weight...]
  transfers between devices with their start and end apart: 10 -> 16, of which waited for: 9 -> 9; matrix products, arithmetic and copies ran while one was open for 1% -> 1% of each run, Pallas kernels for 0% -> 0%
where the time goes in v2:
time: 48.6 us; the launch traced here: 48.4 us
  starting transfers between devices  24.6 us (51%)
  waiting for transfers between devices  13.9 us (29%)
  Pallas kernels  6.07 us (12%)
  local copies, waits for them, and re-layouts  2.03 us (4%)
  between operations  1.46 us (3%)
    ppermute x10, starting transfers between devices, swapped(): return lax.ppermute(block, ('space', 'rep'), route)  17.4 us
    ppermute x10, waiting for transfers between devices, swapped(): return lax.ppermute(block, ('space', 'rep'), route)  10.1 us
    ppermute x1, starting transfers between devices, body(): lax.ppermute(faces, 'space', [(i, i ^ 1) for i in range(strips) if i ^ 1...  5.82 us
    pallas_call x1, Pallas kernels, body(): pl.pallas_call(section_kernel, out_shape=(jax.ShapeDtypeStruct((slots, ch...  4.36 us
    ppermute x4, waiting for transfers between devices, other_core(): lax.ppermute(block, 'rep', [(i, i ^ 1) for i in range(lax.axis_size('rep'...  2.31 us
    pallas_call x1, Pallas kernels, body(): pl.pallas_call(unpack_kernel, out_shape=(jax.ShapeDtypeStruct(conv_weight...  1.7 us
    ppermute x1, waiting for transfers between devices, body(): lax.ppermute(faces, 'space', [(i, i ^ 1) for i in range(strips) if i ^ 1...  1.5 us
    unnamed x10, local copies, waits for them, and re-layouts  1.03 us
  transfers between devices with their start and end apart: 16, of which 9 were waited for; matrix products, arithmetic and copies ran while one was open for 1% of the time, Pallas kernels for 0%

profile of v2, /device:TPU:0, one launch (start us, length us, event | category | flops | bytes accessed | tf_op | source)
XLA Modules:
  0.0 48.4 jit_solution(11595096039143659739)
XLA Ops:
  0.6 1.0 %fusion = (bf16[4,64,64]{2,1,0:T(8,128)(2,1)S(1)}, bf16[4,64,64]{2,1,0:T(8,128)(2,1)S(1)}) fusion(bf16[4,64,512]{2,1,0:T(8,128)(2,1)} %feat_ref.1), kind=kLoop, calls=%fused_computation.8 | loop fusion | bytes 131072 | tf_op jit(solution)/shard_map/slice | solution.py:269
  1.7 0.1 pad_maximum_fusion
  1.8 0.7 %collective-permute-start.1 = (bf16[4,64,128]{2,1,0:T(8,128)(2,1)S(1)}, bf16[4,64,128]{2,1,0:T(8,128)(2,1)S(1)}, u32[]{:S(2)}, u32[]{:S(2)}) collective-permute-start(bf16[4,64,128]{2,1,0:T(8,128)(2,1)S(1)} %pad_maximum_fusion), channel_id=1, source_target_pairs={{4,8},{12,16},{20,24},{8,4},{16,12},{24,20},{5,9},{13,17},{21,25},... | collective-permute-start | bytes 196616 | tf_op jit(solution)/shard_map/ppermute | solution.py:272
  2.4 5.8 %collective-permute-start = (bf16[4,64,128]{2,1,0:T(8,128)(2,1)S(1)}, bf16[4,64,128]{2,1,0:T(8,128)(2,1)S(1)}, u32[]{:S(2)}, u32[]{:S(2)}) collective-permute-start(bf16[4,64,128]{2,1,0:T(8,128)(2,1)S(1)} %pad_maximum_fusion), channel_id=1, source_target_pairs={{0,4},{4,0},{8,12},{12,8},{16,20},{20,16},{24,28},{28,24},{1,5},{5... | collective-permute-start | bytes 196616 | tf_op jit(solution)/shard_map/ppermute | solution.py:270
  8.9 0.1 pad_add_fusion.place_ref
  9.0 1.5 %collective-permute-done.near_ref = bf16[4,64,128]{2,1,0:T(8,128)(2,1)S(1)} collective-permute-done((bf16[4,64,128]{2,1,0:T(8,128)(2,1)S(1)}, bf16[4,64,128]{2,1,0:T(8,128)(2,1)S(1)}, u32[]{:S(2)}, u32[]{:S(2)}) %collective-permute-start) | collective-permute-done | bytes 65568 | tf_op jit(solution)/shard_map/ppermute | solution.py:270
  10.5 1.0 %copy-done.1 = bf16[27,64,64]{2,1,0:T(8,128)(2,1)S(1)} copy-done((bf16[27,64,64]{2,1,0:T(8,128)(2,1)S(1)}, bf16[27,64,64]{2,1,0:T(8,128)(2,1)}, u32[]{:S(2)}) %copy-start.1) | copy-done | bytes 221208
  11.5 4.4 %section.1 = (bf16[4,64,512]{2,1,0:T(8,128)(2,1)}, f32[352,128]{1,0:T(8,128)S(1)}, f32[352,128]{1,0:T(8,128)S(1)}, f32[352,128]{1,0:T(8,128)S(1)}, f32[352,128]{1,0:T(8,128)S(1)}) custom-call(s32[4,27]{1,0:T(4,128)S(1)} %copy-done.4, s32[1]{0:T(128)S(6)} %copy.9.cnt_ref, s32[2]{0:T(128)S(1)} %pad_add_fusion.place_ref, bf16[4,64,512]{2,1,0:T(8,128)(2,1)S(1)} %copy-done, ...), custom_call_target="tpu_custom_call" | custom-call | tf_op jit(solution)/shard_map/section/pallas_call | solution.py:280
  15.9 0.1 collective-permute-start.2
  16.0 0.5 collective-permute-start.9
  16.5 0.9 %collective-permute-done.2 = f32[352,128]{1,0:T(8,128)S(1)} collective-permute-done((f32[352,128]{1,0:T(8,128)S(1)}, f32[352,128]{1,0:T(8,128)S(1)}, u32[]{:S(2)}, u32[]{:S(2)}) %collective-permute-start.2) | collective-permute-done | bytes 180256 | tf_op jit(solution)/shard_map/ppermute | solution.py:233
  17.4 1.6 %collective-permute-start.3 = (f32[176,128]{1,0:T(8,128)S(1)}, f32[176,128]{1,0:T(8,128)S(1)}, u32[]{:S(2)}, u32[]{:S(2)}) collective-permute-start(f32[176,128]{1,0:T(8,128)S(1)} %slice_select_fusion.1), channel_id=1, source_target_pairs={{0,2},{1,5},{2,0},{3,7},{4,6},{5,1},{6,4},{7,3},{8,10},{9,13},{10,... | collective-permute-start | bytes 270344 | tf_op jit(solution)/shard_map/ppermute | solution.py:244
  19.1 0.6 %collective-permute-start.10 = (f32[176,128]{1,0:T(8,128)S(1)}, f32[176,128]{1,0:T(8,128)S(1)}, u32[]{:S(2)}, u32[]{:S(2)}) collective-permute-start(f32[176,128]{1,0:T(8,128)S(1)} %slice_select_fusion), channel_id=1, source_target_pairs={{0,2},{1,5},{2,0},{3,7},{4,6},{5,1},{6,4},{7,3},{8,10},{9,13},{10,... | collective-permute-start | bytes 270344 | tf_op jit(solution)/shard_map/ppermute | solution.py:244
  19.7 2.4 %collective-permute-done.3 = f32[176,128]{1,0:T(8,128)S(1)} collective-permute-done((f32[176,128]{1,0:T(8,128)S(1)}, f32[176,128]{1,0:T(8,128)S(1)}, u32[]{:S(2)}, u32[]{:S(2)}) %collective-permute-start.3) | collective-permute-done | bytes 90144 | tf_op jit(solution)/shard_map/ppermute | solution.py:244
  22.1 2.3 %collective-permute-start.4 = (f32[176,128]{1,0:T(8,128)S(1)}, f32[176,128]{1,0:T(8,128)S(1)}, u32[]{:S(2)}, u32[]{:S(2)}) collective-permute-start(f32[176,128]{1,0:T(8,128)S(1)} %select_add_fusion.1), channel_id=1, source_target_pairs={{0,4},{1,3},{2,6},{3,1},{4,0},{5,7},{6,2},{7,5},{8,12},{9,11},{10,... | collective-permute-start | bytes 270344 | tf_op jit(solution)/shard_map/ppermute | solution.py:244
  24.4 1.6 %collective-permute-start.11 = (f32[176,128]{1,0:T(8,128)S(1)}, f32[176,128]{1,0:T(8,128)S(1)}, u32[]{:S(2)}, u32[]{:S(2)}) collective-permute-start(f32[176,128]{1,0:T(8,128)S(1)} %select_add_fusion), channel_id=1, source_target_pairs={{0,4},{1,3},{2,6},{3,1},{4,0},{5,7},{6,2},{7,5},{8,12},{9,11},{10,... | collective-permute-start | bytes 270344 | tf_op jit(solution)/shard_map/ppermute | solution.py:244
  26.0 0.9 %collective-permute-done.4 = f32[176,128]{1,0:T(8,128)S(1)} collective-permute-done((f32[176,128]{1,0:T(8,128)S(1)}, f32[176,128]{1,0:T(8,128)S(1)}, u32[]{:S(2)}, u32[]{:S(2)}) %collective-permute-start.4) | collective-permute-done | bytes 90144 | tf_op jit(solution)/shard_map/ppermute | solution.py:244
  26.9 2.1 %collective-permute-start.5 = (f32[176,128]{1,0:T(8,128)S(1)}, f32[176,128]{1,0:T(8,128)S(1)}, u32[]{:S(2)}, u32[]{:S(2)}) collective-permute-start(f32[176,128]{1,0:T(8,128)S(1)} %add.32), channel_id=1, source_target_pairs={{0,8},{1,17},{2,10},{3,19},{4,12},{5,21},{6,14},{7,23},{8,0},{9,25... | collective-permute-start | bytes 270344 | tf_op jit(solution)/shard_map/ppermute | solution.py:244
  29.1 1.6 %collective-permute-start.12 = (f32[176,128]{1,0:T(8,128)S(1)}, f32[176,128]{1,0:T(8,128)S(1)}, u32[]{:S(2)}, u32[]{:S(2)}) collective-permute-start(f32[176,128]{1,0:T(8,128)S(1)} %add.37), channel_id=1, source_target_pairs={{0,8},{1,17},{2,10},{3,19},{4,12},{5,21},{6,14},{7,23},{8,0},{9,25... | collective-permute-start | bytes 270344 | tf_op jit(solution)/shard_map/ppermute | solution.py:244
  30.7 1.2 %collective-permute-done.5 = f32[176,128]{1,0:T(8,128)S(1)} collective-permute-done((f32[176,128]{1,0:T(8,128)S(1)}, f32[176,128]{1,0:T(8,128)S(1)}, u32[]{:S(2)}, u32[]{:S(2)}) %collective-permute-start.5) | collective-permute-done | bytes 90144 | tf_op jit(solution)/shard_map/ppermute | solution.py:244
  31.9 3.2 %collective-permute-start.6 = (f32[176,128]{1,0:T(8,128)S(1)}, f32[176,128]{1,0:T(8,128)S(1)}, u32[]{:S(2)}, u32[]{:S(2)}) collective-permute-start(f32[176,128]{1,0:T(8,128)S(1)} %add.33), channel_id=1, source_target_pairs={{0,16},{1,9},{2,18},{3,11},{4,20},{5,13},{6,22},{7,15},{8,24},{9,1... | collective-permute-start | bytes 270344 | tf_op jit(solution)/shard_map/ppermute | solution.py:244
  35.1 1.2 %collective-permute-start.13 = (f32[176,128]{1,0:T(8,128)S(1)}, f32[176,128]{1,0:T(8,128)S(1)}, u32[]{:S(2)}, u32[]{:S(2)}) collective-permute-start(f32[176,128]{1,0:T(8,128)S(1)} %add.38), channel_id=1, source_target_pairs={{0,16},{1,9},{2,18},{3,11},{4,20},{5,13},{6,22},{7,15},{8,24},{9,1... | collective-permute-start | bytes 270344 | tf_op jit(solution)/shard_map/ppermute | solution.py:244
  36.4 1.3 %collective-permute-done.6 = f32[176,128]{1,0:T(8,128)S(1)} collective-permute-done((f32[176,128]{1,0:T(8,128)S(1)}, f32[176,128]{1,0:T(8,128)S(1)}, u32[]{:S(2)}, u32[]{:S(2)}) %collective-permute-start.6) | collective-permute-done | bytes 90144 | tf_op jit(solution)/shard_map/ppermute | solution.py:244
  37.6 1.6 %collective-permute-start.7 = (f32[176,128]{1,0:T(8,128)S(1)}, f32[176,128]{1,0:T(8,128)S(1)}, u32[]{:S(2)}, u32[]{:S(2)}) collective-permute-start(f32[176,128]{1,0:T(8,128)S(1)} %add.34), channel_id=1, source_target_pairs={{0,2},{1,5},{2,0},{3,7},{4,6},{5,1},{6,4},{7,3},{8,10},{9,13},{10,... | collective-permute-start | bytes 270344 | tf_op jit(solution)/shard_map/ppermute | solution.py:244
  39.2 1.4 %collective-permute-done.13 = f32[176,128]{1,0:T(8,128)S(1)} collective-permute-done((f32[176,128]{1,0:T(8,128)S(1)}, f32[176,128]{1,0:T(8,128)S(1)}, u32[]{:S(2)}, u32[]{:S(2)}) %collective-permute-start.13) | collective-permute-done | bytes 90144 | tf_op jit(solution)/shard_map/ppermute | solution.py:244
  40.6 1.6 %collective-permute-start.14 = (f32[176,128]{1,0:T(8,128)S(1)}, f32[176,128]{1,0:T(8,128)S(1)}, u32[]{:S(2)}, u32[]{:S(2)}) collective-permute-start(f32[176,128]{1,0:T(8,128)S(1)} %add.39), channel_id=1, source_target_pairs={{0,2},{1,5},{2,0},{3,7},{4,6},{5,1},{6,4},{7,3},{8,10},{9,13},{10,... | collective-permute-start | bytes 270344 | tf_op jit(solution)/shard_map/ppermute | solution.py:244
  42.2 0.0 collective-permute-done.7
  42.2 0.1 collective-permute-start.8
  42.3 2.9 %collective-permute-done.14 = f32[176,128]{1,0:T(8,128)S(1)} collective-permute-done((f32[176,128]{1,0:T(8,128)S(1)}, f32[176,128]{1,0:T(8,128)S(1)}, u32[]{:S(2)}, u32[]{:S(2)}) %collective-permute-start.14) | collective-permute-done | bytes 90144 | tf_op jit(solution)/shard_map/ppermute | solution.py:244
  45.2 0.1 collective-permute-start.15
  45.3 1.4 %collective-permute-done.15.other_b = f32[352,128]{1,0:T(8,128)S(1)} collective-permute-done((f32[352,128]{1,0:T(8,128)S(1)}, f32[352,128]{1,0:T(8,128)S(1)}, u32[]{:S(2)}, u32[]{:S(2)}) %collective-permute-start.15) | collective-permute-done | bytes 180256 | tf_op jit(solution)/shard_map/ppermute | solution.py:233
  46.7 1.7 %unpack.1 = (f32[27,64,64]{2,1,0:T(8,128)}, f32[8,64,128]{2,1,0:T(8,128)}) custom-call(s32[2]{0:T(128)S(1)} %pad_add_fusion.place_ref, f32[352,128]{1,0:T(8,128)S(1)} %maximum_select_fusion.mine_a, f32[352,128]{1,0:T(8,128)S(1)} %collective-permute-done.8.other_a, f32[352,128]{1,0:T(8,128)S(1)} %maximum_select_fusion.1.mine_b, ...), custom_call_target="tpu_custom_call" | custom-call | tf_op jit(solution)/shard_map/unpack/pallas_call | solution.py:304
  (29 shorter events, 0.3 us)
Async XLA Ops:
  0.6 9.9 %copy-start = (bf16[4,64,512]{2,1,0:T(8,128)(2,1)S(1)}, bf16[4,64,512]{2,1,0:T(8,128)(2,1)}, u32[]{:S(2)}) copy-start(bf16[4,64,512]{2,1,0:T(8,128)(2,1)} %feat_ref.1) | copy-start | bytes 786436
  1.6 8.9 %copy-start.2 = (bf16[8,128,64]{1,2,0:T(8,128)(2,1)S(1)}, bf16[8,128,64]{1,2,0:T(8,128)(2,1)}, u32[]{:S(2)}) copy-start(bf16[8,128,64]{1,2,0:T(8,128)(2,1)} %param.11) | copy-start | bytes 393220
  1.7 8.9 %copy-start.3 = (bf16[4,64,128]{2,1,0:T(8,128)(2,1)S(1)}, bf16[4,64,128]{2,1,0:T(8,128)(2,1)}, u32[]{:S(2)}) copy-start(bf16[4,64,128]{2,1,0:T(8,128)(2,1)} %cot_ref.1) | copy-start | bytes 196612
  1.8 7.2 %collective-permute-start.1 = (bf16[4,64,128]{2,1,0:T(8,128)(2,1)S(1)}, bf16[4,64,128]{2,1,0:T(8,128)(2,1)S(1)}, u32[]{:S(2)}, u32[]{:S(2)}) collective-permute-start(bf16[4,64,128]{2,1,0:T(8,128)(2,1)S(1)} %pad_maximum_fusion), channel_id=1, source_target_pairs={{4,8},{12,16},{20,24},{8,4},{16,12},{24,20},{5,9},{13,17},{21,25},... | collective-permute-start | bytes 196616 | tf_op jit(solution)/shard_map/ppermute | solution.py:272
  2.4 8.1 %collective-permute-start = (bf16[4,64,128]{2,1,0:T(8,128)(2,1)S(1)}, bf16[4,64,128]{2,1,0:T(8,128)(2,1)S(1)}, u32[]{:S(2)}, u32[]{:S(2)}) collective-permute-start(bf16[4,64,128]{2,1,0:T(8,128)(2,1)S(1)} %pad_maximum_fusion), channel_id=1, source_target_pairs={{0,4},{4,0},{8,12},{12,8},{16,20},{20,16},{24,28},{28,24},{1,5},{5... | collective-permute-start | bytes 196616 | tf_op jit(solution)/shard_map/ppermute | solution.py:270
  8.9 1.6 %copy-start.4 = (s32[4,27]{1,0:T(4,128)S(1)}, s32[4,27]{1,0:T(4,128)}, u32[]{:S(2)}) copy-start(s32[4,27]{1,0:T(4,128)} %nb_ref.1) | copy-start | bytes 1300
  10.5 1.0 %copy-start.1 = (bf16[27,64,64]{2,1,0:T(8,128)(2,1)S(1)}, bf16[27,64,64]{2,1,0:T(8,128)(2,1)}, u32[]{:S(2)}) copy-start(bf16[27,64,64]{2,1,0:T(8,128)(2,1)} %cw_ref.1) | copy-start | bytes 663556
  15.9 1.5 %collective-permute-start.2 = (f32[352,128]{1,0:T(8,128)S(1)}, f32[352,128]{1,0:T(8,128)S(1)}, u32[]{:S(2)}, u32[]{:S(2)}) collective-permute-start(f32[352,128]{1,0:T(8,128)S(1)} %get-tuple-element.12), channel_id=1, source_target_pairs={{0,1},{1,0},{2,3},{3,2},{4,5},{5,4},{6,7},{7,6},{8,9},{9,8},{10,11... | collective-permute-start | bytes 540680 | tf_op jit(solution)/shard_map/ppermute | solution.py:233
  16.0 3.0 %collective-permute-start.9 = (f32[352,128]{1,0:T(8,128)S(1)}, f32[352,128]{1,0:T(8,128)S(1)}, u32[]{:S(2)}, u32[]{:S(2)}) collective-permute-start(f32[352,128]{1,0:T(8,128)S(1)} %get-tuple-element.14), channel_id=1, source_target_pairs={{0,1},{1,0},{2,3},{3,2},{4,5},{5,4},{6,7},{7,6},{8,9},{9,8},{10,11... | collective-permute-start | bytes 540680 | tf_op jit(solution)/shard_map/ppermute | solution.py:233
  17.4 4.6 %collective-permute-start.3 = (f32[176,128]{1,0:T(8,128)S(1)}, f32[176,128]{1,0:T(8,128)S(1)}, u32[]{:S(2)}, u32[]{:S(2)}) collective-permute-start(f32[176,128]{1,0:T(8,128)S(1)} %slice_select_fusion.1), channel_id=1, source_target_pairs={{0,2},{1,5},{2,0},{3,7},{4,6},{5,1},{6,4},{7,3},{8,10},{9,13},{10,... | collective-permute-start | bytes 270344 | tf_op jit(solution)/shard_map/ppermute | solution.py:244
  19.1 5.4 %collective-permute-start.10 = (f32[176,128]{1,0:T(8,128)S(1)}, f32[176,128]{1,0:T(8,128)S(1)}, u32[]{:S(2)}, u32[]{:S(2)}) collective-permute-start(f32[176,128]{1,0:T(8,128)S(1)} %slice_select_fusion), channel_id=1, source_target_pairs={{0,2},{1,5},{2,0},{3,7},{4,6},{5,1},{6,4},{7,3},{8,10},{9,13},{10,... | collective-permute-start | bytes 270344 | tf_op jit(solution)/shard_map/ppermute | solution.py:244
  22.1 4.9 %collective-permute-start.4 = (f32[176,128]{1,0:T(8,128)S(1)}, f32[176,128]{1,0:T(8,128)S(1)}, u32[]{:S(2)}, u32[]{:S(2)}) collective-permute-start(f32[176,128]{1,0:T(8,128)S(1)} %select_add_fusion.1), channel_id=1, source_target_pairs={{0,4},{1,3},{2,6},{3,1},{4,0},{5,7},{6,2},{7,5},{8,12},{9,11},{10,... | collective-permute-start | bytes 270344 | tf_op jit(solution)/shard_map/ppermute | solution.py:244
  24.4 4.6 %collective-permute-start.11 = (f32[176,128]{1,0:T(8,128)S(1)}, f32[176,128]{1,0:T(8,128)S(1)}, u32[]{:S(2)}, u32[]{:S(2)}) collective-permute-start(f32[176,128]{1,0:T(8,128)S(1)} %select_add_fusion), channel_id=1, source_target_pairs={{0,4},{1,3},{2,6},{3,1},{4,0},{5,7},{6,2},{7,5},{8,12},{9,11},{10,... | collective-permute-start | bytes 270344 | tf_op jit(solution)/shard_map/ppermute | solution.py:244
  26.9 4.9 %collective-permute-start.5 = (f32[176,128]{1,0:T(8,128)S(1)}, f32[176,128]{1,0:T(8,128)S(1)}, u32[]{:S(2)}, u32[]{:S(2)}) collective-permute-start(f32[176,128]{1,0:T(8,128)S(1)} %add.32), channel_id=1, source_target_pairs={{0,8},{1,17},{2,10},{3,19},{4,12},{5,21},{6,14},{7,23},{8,0},{9,25... | collective-permute-start | bytes 270344 | tf_op jit(solution)/shard_map/ppermute | solution.py:244
  29.1 6.0 %collective-permute-start.12 = (f32[176,128]{1,0:T(8,128)S(1)}, f32[176,128]{1,0:T(8,128)S(1)}, u32[]{:S(2)}, u32[]{:S(2)}) collective-permute-start(f32[176,128]{1,0:T(8,128)S(1)} %add.37), channel_id=1, source_target_pairs={{0,8},{1,17},{2,10},{3,19},{4,12},{5,21},{6,14},{7,23},{8,0},{9,25... | collective-permute-start | bytes 270344 | tf_op jit(solution)/shard_map/ppermute | solution.py:244
  31.9 5.7 %collective-permute-start.6 = (f32[176,128]{1,0:T(8,128)S(1)}, f32[176,128]{1,0:T(8,128)S(1)}, u32[]{:S(2)}, u32[]{:S(2)}) collective-permute-start(f32[176,128]{1,0:T(8,128)S(1)} %add.33), channel_id=1, source_target_pairs={{0,16},{1,9},{2,18},{3,11},{4,20},{5,13},{6,22},{7,15},{8,24},{9,1... | collective-permute-start | bytes 270344 | tf_op jit(solution)/shard_map/ppermute | solution.py:244
  35.1 5.5 %collective-permute-start.13 = (f32[176,128]{1,0:T(8,128)S(1)}, f32[176,128]{1,0:T(8,128)S(1)}, u32[]{:S(2)}, u32[]{:S(2)}) collective-permute-start(f32[176,128]{1,0:T(8,128)S(1)} %add.38), channel_id=1, source_target_pairs={{0,16},{1,9},{2,18},{3,11},{4,20},{5,13},{6,22},{7,15},{8,24},{9,1... | collective-permute-start | bytes 270344 | tf_op jit(solution)/shard_map/ppermute | solution.py:244
  37.6 4.6 %collective-permute-start.7 = (f32[176,128]{1,0:T(8,128)S(1)}, f32[176,128]{1,0:T(8,128)S(1)}, u32[]{:S(2)}, u32[]{:S(2)}) collective-permute-start(f32[176,128]{1,0:T(8,128)S(1)} %add.34), channel_id=1, source_target_pairs={{0,2},{1,5},{2,0},{3,7},{4,6},{5,1},{6,4},{7,3},{8,10},{9,13},{10,... | collective-permute-start | bytes 270344 | tf_op jit(solution)/shard_map/ppermute | solution.py:244
  40.6 4.6 %collective-permute-start.14 = (f32[176,128]{1,0:T(8,128)S(1)}, f32[176,128]{1,0:T(8,128)S(1)}, u32[]{:S(2)}, u32[]{:S(2)}) collective-permute-start(f32[176,128]{1,0:T(8,128)S(1)} %add.39), channel_id=1, source_target_pairs={{0,2},{1,5},{2,0},{3,7},{4,6},{5,1},{6,4},{7,3},{8,10},{9,13},{10,... | collective-permute-start | bytes 270344 | tf_op jit(solution)/shard_map/ppermute | solution.py:244
  42.2 3.1 %collective-permute-start.8 = (f32[352,128]{1,0:T(8,128)S(1)}, f32[352,128]{1,0:T(8,128)S(1)}, u32[]{:S(2)}, u32[]{:S(2)}) collective-permute-start(f32[352,128]{1,0:T(8,128)S(1)} %maximum_select_fusion.mine_a), channel_id=1, source_target_pairs={{0,1},{1,0},{2,3},{3,2},{4,5},{5,4},{6,7},{7,6},{8,9},{9,8},{10,11... | collective-permute-start | bytes 540680 | tf_op jit(solution)/shard_map/ppermute | solution.py:233
  45.2 1.5 %collective-permute-start.15 = (f32[352,128]{1,0:T(8,128)S(1)}, f32[352,128]{1,0:T(8,128)S(1)}, u32[]{:S(2)}, u32[]{:S(2)}) collective-permute-start(f32[352,128]{1,0:T(8,128)S(1)} %maximum_select_fusion.1.mine_b), channel_id=1, source_target_pairs={{0,1},{1,0},{2,3},{3,2},{4,5},{5,4},{6,7},{7,6},{8,9},{9,8},{10,11... | collective-permute-start | bytes 540680 | tf_op jit(solution)/shard_map/ppermute | solution.py:233

commit v3 on v2

--- a/solution.py
+++ b/solution.py
@@ -25,29 +25,28 @@
     return jnp.concatenate([rows, rows], 0).astype(F32).T
 
 
-def section_kernel(
-    nb_ref, cnt_ref, place_ref, feat_ref, near_ref, far_ref, cot_ref, cw_ref, dw_ref,
-    hid_ref, keep_a_ref, give_a_ref, keep_b_ref, give_b_ref,
-    t0_ref, tl_ref, th_ref, sa_ref, sb_ref, wn_ref, hp_ref, as_ref, grad_ref,
-):
-    slots, ch, vox = feat_ref.shape
+def regroup(blocks, outer, inner):
+    ch = half = 64
+    low = lane_iota((ch, LANES)) < half
+
+    rows = []
+    for j in range(inner):
+        tiles = []
+        for m in range(outer // 2):
+            a = blocks[2 * m * ch : (2 * m + 1) * ch, j // 2 * LANES : (j // 2 + 1) * LANES]
+            b = blocks[(2 * m + 1) * ch : (2 * m + 2) * ch, j // 2 * LANES : (j // 2 + 1) * LANES]
+            if j % 2 == 0:
+                tiles.append(jnp.where(low, a, pltpu.roll(b, half, 1)))
+            else:
+                tiles.append(jnp.where(low, pltpu.roll(a, half, 1), b))
+        rows.append(jnp.concatenate(tiles, 1))
+    return jnp.concatenate(rows, 0)
+
+
+def weights_kernel(cw_ref, cot_ref, dw_ref, wn_ref, onehot_ref, hp_ref):
+    ch, vox = cw_ref.shape[-1], onehot_ref.shape[0]
+    slots = cot_ref.shape[0]
     half = ch
-    odd = place_ref[0]
-    core = place_ref[1]
-
-    t0_ref[slots] = jnp.zeros(t0_ref.shape[1:], F32)
-    tl_ref[2 * slots] = jnp.zeros(tl_ref.shape[1:], F32)
-    th_ref[2 * slots] = jnp.zeros(th_ref.shape[1:], F32)
-    for j in range(slots):
-        block = doubled(feat_ref[j]).reshape(8, 8, 8, LANES)
-        t0_ref[j] = block
-        tl_ref[j] = block[7]
-        th_ref[j] = block[0]
-        near, far = doubled(near_ref[j]), doubled(far_ref[j])
-        before = jnp.where(odd == 1, near, far)
-        after = jnp.where(odd == 1, far, near)
-        tl_ref[slots + j] = before[64:].reshape(8, 8, LANES)
-        th_ref[slots + j] = after[:64].reshape(8, 8, LANES)
 
     low_lanes = lane_iota((ch, LANES)) < half
     for iy in range(3):
@@ -68,44 +67,51 @@
         + 2 * (u % 4) + t % 2
     )
     lane = lane_iota((vox, LANES))
-    onehot = jnp.concatenate(
-        [
-            jnp.where(voxel == lane + q * LANES, 1.0, 0.0).astype(BF16)
-            for q in range(vox // LANES)
-        ],
-        1,
-    )
+    for q in range(vox // LANES):
+        hot = jnp.where(voxel == lane + q * LANES, 1.0, 0.0)
+        onehot_ref[:, pl.ds(q * LANES, LANES)] = hot.astype(BF16)
 
     cot = cot_ref[...].reshape(slots * 64, LANES)
     taps = dw_ref.shape[0]
     hg = dot(dw_ref[...].reshape(taps * ch, LANES), cot, ((1,), (1,)))
-    low = lane_iota((ch, LANES)) < half
-
-    def regroup(blocks, outer, inner):
-        rows = []
-        for j in range(inner):
-            tiles = []
-            for m in range(outer // 2):
-                a = blocks[2 * m * ch : (2 * m + 1) * ch, j // 2 * LANES : (j // 2 + 1) * LANES]
-                b = blocks[(2 * m + 1) * ch : (2 * m + 2) * ch, j // 2 * LANES : (j // 2 + 1) * LANES]
-                if j % 2 == 0:
-                    tiles.append(jnp.where(low, a, pltpu.roll(b, half, 1)))
-                else:
-                    tiles.append(jnp.where(low, pltpu.roll(a, half, 1), b))
-            rows.append(jnp.concatenate(tiles, 1))
-        return jnp.concatenate(rows, 0)
 
     hg = regroup(hg, taps, slots).astype(BF16)
-    hp_ref[...] = dot(hg, onehot, ((1,), (0,)))
+    hp_ref[...] = dot(hg, onehot_ref[...], ((1,), (0,))).astype(BF16)
+
+
+def section_kernel(
+    info_ref, feat_ref, near_ref, far_ref, cot_ref, wn_ref, onehot_ref, hp_ref,
+    hid_ref, keep_a_ref, give_a_ref, keep_b_ref, give_b_ref,
+    t0_ref, tl_ref, th_ref, sa_ref, sb_ref, as_ref, grad_ref,
+):
+    slots, ch, vox = feat_ref.shape
+    half = ch
+    odd, core = info_ref[0], info_ref[1]
+
+    t0_ref[slots] = jnp.zeros(t0_ref.shape[1:], F32)
+    tl_ref[2 * slots] = jnp.zeros(tl_ref.shape[1:], F32)
+    th_ref[2 * slots] = jnp.zeros(th_ref.shape[1:], F32)
+    for j in range(slots):
+        block = doubled(feat_ref[j]).reshape(8, 8, 8, LANES)
+        t0_ref[j] = block
+        tl_ref[j] = block[7]
+        th_ref[j] = block[0]
+    near = near_ref[...].reshape(LANES, LANES).astype(F32).T
+    far = far_ref[...].reshape(LANES, LANES).astype(F32).T
+    narrow = lane_iota((64, LANES)) < half
+    for side, table in ((1, tl_ref), (0, th_ref)):
+        planes = jnp.where(odd == side, near, far)
+        turned = pltpu.roll(planes, half, 1)
+        for j in range(slots):
+            rows = slice(j // 2 * 64, (j // 2 + 1) * 64)
+            a, b = (planes, turned) if j % 2 == 0 else (turned, planes)
+            table[slots + j] = jnp.where(narrow, a[rows], b[rows]).reshape(8, 8, LANES)
+
+    cot = cot_ref[...].reshape(slots * 64, LANES)
 
     zi = lax.broadcasted_iota(jnp.int32, (10, 8, LANES), 1)
     li = lane_iota((10, 8, LANES))
     for j in range(slots):
-        def source(col):
-            n = nb_ref[j, col]
-            return jnp.where(n < 0, slots if 9 <= col < 18 else 2 * slots, n)
-
-        centre = jnp.where(j < cnt_ref[0], j, slots)
         for xp in range(10):
             ox = -1 if xp == 0 else (1 if xp == 9 else 0)
             shifted = []
@@ -113,7 +119,11 @@
                 pieces = []
                 for oy in (-1, 0, 1):
                     col = (ox + 1) * 9 + (oy + 1) * 3 + oz + 1
-                    n = centre if col == 13 else source(col)
+                    if col == 13:
+                        n = jnp.where(j < info_ref[2], j, slots)
+                    else:
+                        n = info_ref[3 + j * 27 + col]
+                        n = jnp.where(n < 0, slots if ox == 0 else 2 * slots, n)
                     ys = slice(7, 8) if oy < 0 else (slice(0, 1) if oy > 0 else slice(0, 8))
                     if ox == 0:
                         pieces.append(t0_ref[n, xp - 1, ys])
@@ -139,27 +149,35 @@
         return s.reshape(count * 640, 2 * LANES)
 
     zero = jnp.zeros((ch, LANES), F32)
-    for j in range(slots):
-        out = dot(window(0, j, 1), wn_ref[0], ((1,), (1,)))
-        out = out + dot(window(1, j, 1), wn_ref[1], ((1,), (1,)))
-        out = out + dot(window(2, j, 1), wn_ref[2], ((1,), (1,)))
-        first = out[:, :LANES]
-        second = out[:, LANES:]
-        pre = (
-            first[:vox]
-            + pltpu.roll(first[64 : 64 + vox], half, 1)
-            + jnp.concatenate([second[128 : 128 + vox], jnp.zeros((vox, LANES - ch), F32)], 1)
-        )
-        pre = pre.T[:ch]
-        hid_ref[j] = jnp.maximum(pre, 0.0).astype(BF16)
-        act = jnp.where(pre > 0, hp_ref[pl.ds(j * ch, ch), :], 0.0)
-        lead = jnp.concatenate([act, zero], 1)
-        as_ref[pl.ds(0, ch), pl.ds(j * 640, 640)] = lead.astype(BF16)
-        as_ref[pl.ds(ch, ch), pl.ds(j * 640, 640)] = pltpu.roll(lead, half, 1).astype(BF16)
-        as_ref[pl.ds(2 * ch, ch), pl.ds(j * 640, 640)] = jnp.concatenate([zero, act], 1).astype(BF16)
-
+    wide = lane_iota((vox, LANES)) < half
+    for pair in range(slots // 2):
+        sums = []
+        for j in (2 * pair, 2 * pair + 1):
+            out = dot(window(0, j, 1), wn_ref[0], ((1,), (1,)))
+            out = out + dot(window(1, j, 1), wn_ref[1], ((1,), (1,)))
+            out = out + dot(window(2, j, 1), wn_ref[2], ((1,), (1,)))
+            mid = out[64 : 64 + vox, :LANES]
+            last = out[128 : 128 + vox, LANES:]
+            ends = out[:vox, :LANES] + jnp.concatenate([last, jnp.zeros((vox, LANES - ch), F32)], 1)
+            sums.append((ends, mid))
+        both = jnp.where(
+            wide,
+            sums[0][0] + pltpu.roll(sums[0][1], half, 1),
+            pltpu.roll(sums[1][0], half, 1) + sums[1][1],
+        ).T
+        for j in (2 * pair, 2 * pair + 1):
+            pre = both[j % 2 * ch : (j % 2 + 1) * ch]
+            hid_ref[j] = jnp.maximum(pre, 0.0).astype(BF16)
+            act = jnp.where(pre > 0, hp_ref[pl.ds(j * ch, ch), :].astype(F32), 0.0)
+            lead = jnp.concatenate([act, zero], 1)
+            cols = pl.ds(j * 640, 640)
+            as_ref[pl.ds(0, ch), cols] = lead.astype(BF16)
+            as_ref[pl.ds(ch, ch), cols] = pltpu.roll(lead, half, 1).astype(BF16)
+            as_ref[pl.ds(2 * ch, ch), cols] = jnp.concatenate([zero, act], 1).astype(BF16)
+
+    taps = vox // 64
     hidden = hid_ref[...].reshape(slots * ch, vox)
-    hperm = dot(hidden, onehot, ((1,), (1,)))
+    hperm = dot(hidden, onehot_ref[...], ((1,), (1,)))
     hperm = regroup(hperm, slots, taps).astype(BF16)
     base = 3 * 3 * ch + 3 * ch + 3 * ch // 2
     grad_ref[pl.ds(base, taps * ch), :] = dot(hperm, cot, ((1,), (0,)))
@@ -184,10 +202,10 @@
     give_b_ref[...] = grad_ref[pl.ds(2 * rows + theirs, rows), :]
 
 
-def unpack_kernel(place_ref, mine_a, other_a, mine_b, other_b, conv_ref, down_ref, x_ref):
+def unpack_kernel(info_ref, mine_a, other_a, mine_b, other_b, conv_ref, down_ref, x_ref):
     taps, ch, outs = down_ref.shape
     half = ch
-    core = place_ref[1]
+    core = info_ref[1]
     rows = mine_a.shape[0]
     mine, theirs = pl.multiple_of(core * rows, 8), pl.multiple_of((1 - core) * rows, 8)
     x_ref[pl.ds(mine, rows), :] = mine_a[...]
@@ -266,21 +284,43 @@
 def body(features, neighbours, counts, cotangent, conv_weight, down_weight):
     slots, ch, vox = features.shape
     strips = lax.axis_size("space")
-    faces = jnp.concatenate([features[:, :, :64], features[:, :, vox - 64 :]], 2)
-    near = lax.ppermute(faces, "space", [(i, i ^ 1) for i in range(strips) if i ^ 1 < strips])
+    taps, outs, _ = down_weight.shape
+    odd = lax.axis_index("space") & 1
+    core = lax.axis_index("rep") & 1
+
+    own = jnp.stack([odd, core]).astype(jnp.int32)
+    info = jnp.concatenate([own, counts, neighbours.reshape(-1)])
+
+    pairs = slots // 2
+    lower = jnp.concatenate([features[:pairs, :, :64], features[pairs:, :, :64]], 2)
+    upper = jnp.concatenate([features[:pairs, :, vox - 64 :], features[pairs:, :, vox - 64 :]], 2)
+    steps = [(i, i + 1) for i in range(0, strips - 1, 2)]
+    near = lax.ppermute(jnp.where(odd == 1, lower, upper), "space", steps + [(b, a) for a, b in steps])
     steps = [(i, i + 1) for i in range(1, strips - 1, 2)]
-    far = lax.ppermute(faces, "space", steps + [(b, a) for a, b in steps])
-    place = jnp.stack([lax.axis_index("space") & 1, lax.axis_index("rep") & 1]).astype(jnp.int32)
+    far = lax.ppermute(jnp.where(odd == 1, upper, lower), "space", steps + [(b, a) for a, b in steps])
+
     vmem = pl.BlockSpec(memory_space=pltpu.VMEM)
     smem = pl.BlockSpec(memory_space=pltpu.SMEM)
-    taps, outs, _ = down_weight.shape
+    weights, onehot, mixed = pl.pallas_call(
+        weights_kernel,
+        out_shape=(
+            jax.ShapeDtypeStruct((3, 3 * ch, 2 * LANES), BF16),
+            jax.ShapeDtypeStruct((vox, vox), BF16),
+            jax.ShapeDtypeStruct((slots * ch, vox), BF16),
+        ),
+        in_specs=[vmem] * 3,
+        out_specs=(vmem,) * 3,
+        compiler_params=pltpu.CompilerParams(vmem_limit_bytes=16 << 20),
+        cost_estimate=pl.CostEstimate(flops=10**9, bytes_accessed=10**6, transcendentals=0),
+        name="weights",
+    )(conv_weight, cotangent, jnp.swapaxes(down_weight, 1, 2))
     total = conv_weight.size + down_weight.size
     rows = -(-total // (LANES * 128)) * 128
     part = jax.ShapeDtypeStruct((rows // 4, LANES), F32)
     hidden, keep_a, give_a, keep_b, give_b = pl.pallas_call(
         section_kernel,
         out_shape=(jax.ShapeDtypeStruct((slots, ch, vox), BF16), part, part, part, part),
-        in_specs=[smem] * 3 + [vmem] * 6,
+        in_specs=[smem] + [vmem] * 7,
         out_specs=(vmem,) * 5,
         scratch_shapes=[
             pltpu.VMEM((slots + 1, 8, 8, 8, LANES), F32),
@@ -288,16 +328,13 @@
             pltpu.VMEM((2 * slots + 1, 8, 8, LANES), F32),
             pltpu.VMEM((slots, 10, 80, 2 * LANES), BF16),
             pltpu.VMEM((slots, 10, 64, 2 * LANES), BF16),
-            pltpu.VMEM((3, 3 * ch, 2 * LANES), BF16),
-            pltpu.VMEM((slots * ch, vox), F32),
             pltpu.VMEM((3 * ch, slots * 640), BF16),
             pltpu.VMEM((rows, LANES), F32),
         ],
         compiler_params=pltpu.CompilerParams(vmem_limit_bytes=32 << 20),
         name="section",
     )(
-        neighbours, counts, place, features, near, far, cotangent, conv_weight,
-        jnp.swapaxes(down_weight, 1, 2),
+        info, features, near, far, cotangent, weights, onehot, mixed,
     )
     mine_a = summed(keep_a, give_a)
     mine_b = summed(keep_b, give_b)
@@ -312,7 +349,7 @@
         scratch_shapes=[pltpu.VMEM((rows, LANES), F32)],
         compiler_params=pltpu.CompilerParams(vmem_limit_bytes=16 << 20),
         name="unpack",
-    )(place, mine_a, other_core(mine_a), mine_b, other_core(mine_b))
+    )(info, mine_a, other_core(mine_a), mine_b, other_core(mine_b))
     return hidden, conv_grad, jnp.swapaxes(down_grad, 1, 2)
 
 

time: 48.6 us -> 46.5 us (0.957)
  starting transfers between devices: 24.6 us -> 22.2 us
    ppermute x10, starting transfers between devices: 17.4 us -> 15 us  [swapped(): return lax.ppermute(block, ('space', 'rep'), route)]
    ppermute x2, waiting for transfers between devices: 1.5 us -> 0.01 us  [the longest x1 0.01 us: body(): lax.ppermute(jnp.where(odd == 1, lower, upper), 'space', steps + [(b, a)...]
    ppermute x10, waiting for transfers between devices: 10.1 us -> 11.5 us  [swapped(): return lax.ppermute(block, ('space', 'rep'), route)]
    pallas_call x0 -> x1, Pallas kernels: none -> 0.92 us  [body(): pl.pallas_call(weights_kernel, out_shape=(jax.ShapeDtypeStruct((3, 3 * ch...]
    pallas_call x1, Pallas kernels: 4.36 us -> 3.65 us  [body(): pl.pallas_call(section_kernel, out_shape=(jax.ShapeDtypeStruct((slots, ch...]
  transfers between devices with their start and end apart: 16 -> 16, of which waited for: 9 -> 11; matrix products, arithmetic and copies ran while one was open for 1% -> 1% of each run, Pallas kernels for 0% -> 2%
where the time goes in v3:
time: 46.5 us; the launch traced here: 46.2 us
  starting transfers between devices  22.2 us (48%)
  waiting for transfers between devices  13.9 us (30%)
  Pallas kernels  6.27 us (13%)
  local copies, waits for them, and re-layouts  2.03 us (4%)
  between operations  1.48 us (3%)
    ppermute x10, starting transfers between devices, swapped(): return lax.ppermute(block, ('space', 'rep'), route)  15 us
    ppermute x10, waiting for transfers between devices, swapped(): return lax.ppermute(block, ('space', 'rep'), route)  11.5 us
    ppermute x1, starting transfers between devices, body(): lax.ppermute(jnp.where(odd == 1, lower, upper), 'space', steps + [(b, a)...  5.83 us
    pallas_call x1, Pallas kernels, body(): pl.pallas_call(section_kernel, out_shape=(jax.ShapeDtypeStruct((slots, ch...  3.65 us
    ppermute x4, waiting for transfers between devices, other_core(): lax.ppermute(block, 'rep', [(i, i ^ 1) for i in range(lax.axis_size('rep'...  2.31 us
    pallas_call x1, Pallas kernels, body(): pl.pallas_call(unpack_kernel, out_shape=(jax.ShapeDtypeStruct(conv_weight...  1.7 us
    unnamed x10, local copies, waits for them, and re-layouts  1.05 us
  transfers between devices with their start and end apart: 16, of which 11 were waited for; matrix products, arithmetic and copies ran while one was open for 1% of the time, Pallas kernels for 2%

profile of v3, /device:TPU:0, one launch (start us, length us, event | category | flops | bytes accessed | tf_op | source)
XLA Modules:
  0.0 46.2 jit_solution(4050743008461131774)
XLA Ops:
  0.6 0.9 %fusion = (bf16[2,64,64]{2,1,0:T(8,128)(2,1)S(1)}, bf16[2,64,64]{2,1,0:T(8,128)(2,1)S(1)}, bf16[2,64,64]{2,1,0:T(8,128)(2,1)S(1)}, bf16[2,64,64]{2,1,0:T(8,128)(2,1)S(1)}) fusion(bf16[4,64,512]{2,1,0:T(8,128)(2,1)} %feat_ref.1), kind=kLoop, calls=%fused_computation.11 | loop fusion | bytes 131072 | tf_op jit(solution)/shard_map/slice | solution.py:295
  1.6 0.1 broadcast_select_fusion
  1.7 0.7 %collective-permute-start.1 = (bf16[2,64,128]{2,1,0:T(8,128)(2,1)S(1)}, bf16[2,64,128]{2,1,0:T(8,128)(2,1)S(1)}, u32[]{:S(2)}, u32[]{:S(2)}) collective-permute-start(bf16[2,64,128]{2,1,0:T(8,128)(2,1)S(1)} %get-tuple-element.27), channel_id=1, source_target_pairs={{4,8},{12,16},{20,24},{8,4},{16,12},{24,20},{5,9},{13,17},{21,25},... | collective-permute-start | bytes 98312 | tf_op jit(solution)/shard_map/ppermute | solution.py:300
  2.3 5.8 %collective-permute-start = (bf16[2,64,128]{2,1,0:T(8,128)(2,1)S(1)}, bf16[2,64,128]{2,1,0:T(8,128)(2,1)S(1)}, u32[]{:S(2)}, u32[]{:S(2)}) collective-permute-start(bf16[2,64,128]{2,1,0:T(8,128)(2,1)S(1)} %get-tuple-element.28), channel_id=1, source_target_pairs={{0,4},{8,12},{16,20},{24,28},{4,0},{12,8},{20,16},{28,24},{1,5},{9... | collective-permute-start | bytes 98312 | tf_op jit(solution)/shard_map/ppermute | solution.py:298
  8.8 0.1 reshape.9
  8.9 0.1 pad_add_fusion.info_ref
  9.0 1.0 %copy-done.2 = bf16[27,64,64]{2,1,0:T(8,128)(2,1)S(1)} copy-done((bf16[27,64,64]{2,1,0:T(8,128)(2,1)S(1)}, bf16[27,64,64]{2,1,0:T(8,128)(2,1)}, u32[]{:S(2)}) %copy-start.2) | copy-done | bytes 221208
  10.0 0.9 %weights.1 = (bf16[3,192,256]{2,1,0:T(8,128)(2,1)S(1)}, bf16[512,512]{1,0:T(8,128)(2,1)S(1)}, bf16[256,512]{1,0:T(8,128)(2,1)S(1)}) custom-call(bf16[27,64,64]{2,1,0:T(8,128)(2,1)S(1)} %copy-done.2, bf16[4,64,128]{2,1,0:T(8,128)(2,1)S(1)} %copy-done.1, bf16[8,64,128]{2,1,0:T(8,128)(2,1)S(1)} %bitcast.4), custom_call_target="tpu_custom_call" | custom-call | flops 1000000000 | bytes 1000000 | tf_op jit(solution)/shard_map/weights/pallas_call | solution.py:304
  11.0 3.6 %section.1 = (bf16[4,64,512]{2,1,0:T(8,128)(2,1)}, f32[352,128]{1,0:T(8,128)S(1)}, f32[352,128]{1,0:T(8,128)S(1)}, f32[352,128]{1,0:T(8,128)S(1)}, f32[352,128]{1,0:T(8,128)S(1)}) custom-call(s32[111]{0:T(128)S(1)} %pad_add_fusion.info_ref, bf16[4,64,512]{2,1,0:T(8,128)(2,1)S(1)} %copy-done, bf16[2,64,128]{2,1,0:T(8,128)(2,1)S(1)} %collective-permute-done.near_ref, ...), custom_call_target="tpu_custom_call" | custom-call | tf_op jit(solution)/shard_map/section/pallas_call | solution.py:320
  14.7 0.5 %collective-permute-start.9 = (f32[352,128]{1,0:T(8,128)S(1)}, f32[352,128]{1,0:T(8,128)S(1)}, u32[]{:S(2)}, u32[]{:S(2)}) collective-permute-start(f32[352,128]{1,0:T(8,128)S(1)} %get-tuple-element.20), channel_id=1, source_target_pairs={{0,1},{1,0},{2,3},{3,2},{4,5},{5,4},{6,7},{7,6},{8,9},{9,8},{10,11... | collective-permute-start | bytes 540680 | tf_op jit(solution)/shard_map/ppermute | solution.py:251
  15.2 0.9 %collective-permute-done.2 = f32[352,128]{1,0:T(8,128)S(1)} collective-permute-done((f32[352,128]{1,0:T(8,128)S(1)}, f32[352,128]{1,0:T(8,128)S(1)}, u32[]{:S(2)}, u32[]{:S(2)}) %collective-permute-start.2) | collective-permute-done | bytes 180256 | tf_op jit(solution)/shard_map/ppermute | solution.py:251
  16.2 1.5 %collective-permute-start.3 = (f32[176,128]{1,0:T(8,128)S(1)}, f32[176,128]{1,0:T(8,128)S(1)}, u32[]{:S(2)}, u32[]{:S(2)}) collective-permute-start(f32[176,128]{1,0:T(8,128)S(1)} %slice_select_fusion.1), channel_id=1, source_target_pairs={{0,2},{1,5},{2,0},{3,7},{4,6},{5,1},{6,4},{7,3},{8,10},{9,13},{10,... | collective-permute-start | bytes 270344 | tf_op jit(solution)/shard_map/ppermute | solution.py:262
  17.8 0.6 %collective-permute-start.10 = (f32[176,128]{1,0:T(8,128)S(1)}, f32[176,128]{1,0:T(8,128)S(1)}, u32[]{:S(2)}, u32[]{:S(2)}) collective-permute-start(f32[176,128]{1,0:T(8,128)S(1)} %slice_select_fusion), channel_id=1, source_target_pairs={{0,2},{1,5},{2,0},{3,7},{4,6},{5,1},{6,4},{7,3},{8,10},{9,13},{10,... | collective-permute-start | bytes 270344 | tf_op jit(solution)/shard_map/ppermute | solution.py:262
  18.4 2.4 %collective-permute-done.3 = f32[176,128]{1,0:T(8,128)S(1)} collective-permute-done((f32[176,128]{1,0:T(8,128)S(1)}, f32[176,128]{1,0:T(8,128)S(1)}, u32[]{:S(2)}, u32[]{:S(2)}) %collective-permute-start.3) | collective-permute-done | bytes 90144 | tf_op jit(solution)/shard_map/ppermute | solution.py:262
  20.8 1.1 %collective-permute-start.4 = (f32[176,128]{1,0:T(8,128)S(1)}, f32[176,128]{1,0:T(8,128)S(1)}, u32[]{:S(2)}, u32[]{:S(2)}) collective-permute-start(f32[176,128]{1,0:T(8,128)S(1)} %select_add_fusion.1), channel_id=1, source_target_pairs={{0,4},{1,3},{2,6},{3,1},{4,0},{5,7},{6,2},{7,5},{8,12},{9,11},{10,... | collective-permute-start | bytes 270344 | tf_op jit(solution)/shard_map/ppermute | solution.py:262
  21.9 0.4 collective-permute-done.10
  22.4 1.2 %collective-permute-start.11 = (f32[176,128]{1,0:T(8,128)S(1)}, f32[176,128]{1,0:T(8,128)S(1)}, u32[]{:S(2)}, u32[]{:S(2)}) collective-permute-start(f32[176,128]{1,0:T(8,128)S(1)} %select_add_fusion), channel_id=1, source_target_pairs={{0,4},{1,3},{2,6},{3,1},{4,0},{5,7},{6,2},{7,5},{8,12},{9,11},{10,... | collective-permute-start | bytes 270344 | tf_op jit(solution)/shard_map/ppermute | solution.py:262
  23.5 1.8 %collective-permute-done.4 = f32[176,128]{1,0:T(8,128)S(1)} collective-permute-done((f32[176,128]{1,0:T(8,128)S(1)}, f32[176,128]{1,0:T(8,128)S(1)}, u32[]{:S(2)}, u32[]{:S(2)}) %collective-permute-start.4) | collective-permute-done | bytes 90144 | tf_op jit(solution)/shard_map/ppermute | solution.py:262
  25.4 1.7 %collective-permute-start.5 = (f32[176,128]{1,0:T(8,128)S(1)}, f32[176,128]{1,0:T(8,128)S(1)}, u32[]{:S(2)}, u32[]{:S(2)}) collective-permute-start(f32[176,128]{1,0:T(8,128)S(1)} %add.32), channel_id=1, source_target_pairs={{0,8},{1,17},{2,10},{3,19},{4,12},{5,21},{6,14},{7,23},{8,0},{9,25... | collective-permute-start | bytes 270344 | tf_op jit(solution)/shard_map/ppermute | solution.py:262
  27.1 1.6 %collective-permute-start.12 = (f32[176,128]{1,0:T(8,128)S(1)}, f32[176,128]{1,0:T(8,128)S(1)}, u32[]{:S(2)}, u32[]{:S(2)}) collective-permute-start(f32[176,128]{1,0:T(8,128)S(1)} %add.37), channel_id=1, source_target_pairs={{0,8},{1,17},{2,10},{3,19},{4,12},{5,21},{6,14},{7,23},{8,0},{9,25... | collective-permute-start | bytes 270344 | tf_op jit(solution)/shard_map/ppermute | solution.py:262
  28.6 1.9 %collective-permute-done.5 = f32[176,128]{1,0:T(8,128)S(1)} collective-permute-done((f32[176,128]{1,0:T(8,128)S(1)}, f32[176,128]{1,0:T(8,128)S(1)}, u32[]{:S(2)}, u32[]{:S(2)}) %collective-permute-start.5) | collective-permute-done | bytes 90144 | tf_op jit(solution)/shard_map/ppermute | solution.py:262
  30.6 2.1 %collective-permute-start.6 = (f32[176,128]{1,0:T(8,128)S(1)}, f32[176,128]{1,0:T(8,128)S(1)}, u32[]{:S(2)}, u32[]{:S(2)}) collective-permute-start(f32[176,128]{1,0:T(8,128)S(1)} %add.33), channel_id=1, source_target_pairs={{0,16},{1,9},{2,18},{3,11},{4,20},{5,13},{6,22},{7,15},{8,24},{9,1... | collective-permute-start | bytes 270344 | tf_op jit(solution)/shard_map/ppermute | solution.py:262
  32.7 0.2 collective-permute-done.12
  32.9 2.2 %collective-permute-start.13 = (f32[176,128]{1,0:T(8,128)S(1)}, f32[176,128]{1,0:T(8,128)S(1)}, u32[]{:S(2)}, u32[]{:S(2)}) collective-permute-start(f32[176,128]{1,0:T(8,128)S(1)} %add.38), channel_id=1, source_target_pairs={{0,16},{1,9},{2,18},{3,11},{4,20},{5,13},{6,22},{7,15},{8,24},{9,1... | collective-permute-start | bytes 270344 | tf_op jit(solution)/shard_map/ppermute | solution.py:262
  35.1 1.0 %collective-permute-done.6 = f32[176,128]{1,0:T(8,128)S(1)} collective-permute-done((f32[176,128]{1,0:T(8,128)S(1)}, f32[176,128]{1,0:T(8,128)S(1)}, u32[]{:S(2)}, u32[]{:S(2)}) %collective-permute-start.6) | collective-permute-done | bytes 90144 | tf_op jit(solution)/shard_map/ppermute | solution.py:262
  36.1 1.7 %collective-permute-start.7 = (f32[176,128]{1,0:T(8,128)S(1)}, f32[176,128]{1,0:T(8,128)S(1)}, u32[]{:S(2)}, u32[]{:S(2)}) collective-permute-start(f32[176,128]{1,0:T(8,128)S(1)} %add.34), channel_id=1, source_target_pairs={{0,2},{1,5},{2,0},{3,7},{4,6},{5,1},{6,4},{7,3},{8,10},{9,13},{10,... | collective-permute-start | bytes 270344 | tf_op jit(solution)/shard_map/ppermute | solution.py:262
  37.7 0.7 %collective-permute-done.13 = f32[176,128]{1,0:T(8,128)S(1)} collective-permute-done((f32[176,128]{1,0:T(8,128)S(1)}, f32[176,128]{1,0:T(8,128)S(1)}, u32[]{:S(2)}, u32[]{:S(2)}) %collective-permute-start.13) | collective-permute-done | bytes 90144 | tf_op jit(solution)/shard_map/ppermute | solution.py:262
  38.4 1.4 %collective-permute-start.14 = (f32[176,128]{1,0:T(8,128)S(1)}, f32[176,128]{1,0:T(8,128)S(1)}, u32[]{:S(2)}, u32[]{:S(2)}) collective-permute-start(f32[176,128]{1,0:T(8,128)S(1)} %add.39), channel_id=1, source_target_pairs={{0,2},{1,5},{2,0},{3,7},{4,6},{5,1},{6,4},{7,3},{8,10},{9,13},{10,... | collective-permute-start | bytes 270344 | tf_op jit(solution)/shard_map/ppermute | solution.py:262
  39.8 0.9 %collective-permute-done.7 = f32[176,128]{1,0:T(8,128)S(1)} collective-permute-done((f32[176,128]{1,0:T(8,128)S(1)}, f32[176,128]{1,0:T(8,128)S(1)}, u32[]{:S(2)}, u32[]{:S(2)}) %collective-permute-start.7) | collective-permute-done | bytes 90144 | tf_op jit(solution)/shard_map/ppermute | solution.py:262
  40.8 2.3 %collective-permute-done.14 = f32[176,128]{1,0:T(8,128)S(1)} collective-permute-done((f32[176,128]{1,0:T(8,128)S(1)}, f32[176,128]{1,0:T(8,128)S(1)}, u32[]{:S(2)}, u32[]{:S(2)}) %collective-permute-start.14) | collective-permute-done | bytes 90144 | tf_op jit(solution)/shard_map/ppermute | solution.py:262
  43.1 1.4 %collective-permute-done.15.other_b = f32[352,128]{1,0:T(8,128)S(1)} collective-permute-done((f32[352,128]{1,0:T(8,128)S(1)}, f32[352,128]{1,0:T(8,128)S(1)}, u32[]{:S(2)}, u32[]{:S(2)}) %collective-permute-start.15) | collective-permute-done | bytes 180256 | tf_op jit(solution)/shard_map/ppermute | solution.py:251
  44.5 1.7 %unpack.1 = (f32[27,64,64]{2,1,0:T(8,128)}, f32[8,64,128]{2,1,0:T(8,128)}) custom-call(s32[111]{0:T(128)S(1)} %pad_add_fusion.info_ref, f32[352,128]{1,0:T(8,128)S(1)} %maximum_select_fusion.mine_a, f32[352,128]{1,0:T(8,128)S(1)} %collective-permute-done.8.other_a, f32[352,128]{1,0:T(8,128)S(1)} %maximum_select_fusion.1.mine_b, ...), custom_call_target="tpu_custom_call" | custom-call | tf_op jit(solution)/shard_map/unpack/pallas_call | solution.py:341
  (31 shorter events, 0.5 us)
Async XLA Ops:
  1.5 7.5 %copy-start.3 = (bf16[8,128,64]{1,2,0:T(8,128)(2,1)S(1)}, bf16[8,128,64]{1,2,0:T(8,128)(2,1)}, u32[]{:S(2)}) copy-start(bf16[8,128,64]{1,2,0:T(8,128)(2,1)} %param.11) | copy-start | bytes 393220
  1.6 7.5 %copy-start.1 = (bf16[4,64,128]{2,1,0:T(8,128)(2,1)S(1)}, bf16[4,64,128]{2,1,0:T(8,128)(2,1)}, u32[]{:S(2)}) copy-start(bf16[4,64,128]{2,1,0:T(8,128)(2,1)} %cot_ref.3) | copy-start | bytes 196612
  1.7 9.3 %collective-permute-start.1 = (bf16[2,64,128]{2,1,0:T(8,128)(2,1)S(1)}, bf16[2,64,128]{2,1,0:T(8,128)(2,1)S(1)}, u32[]{:S(2)}, u32[]{:S(2)}) collective-permute-start(bf16[2,64,128]{2,1,0:T(8,128)(2,1)S(1)} %get-tuple-element.27), channel_id=1, source_target_pairs={{4,8},{12,16},{20,24},{8,4},{16,12},{24,20},{5,9},{13,17},{21,25},... | collective-permute-start | bytes 98312 | tf_op jit(solution)/shard_map/ppermute | solution.py:300
  2.3 8.6 %collective-permute-start = (bf16[2,64,128]{2,1,0:T(8,128)(2,1)S(1)}, bf16[2,64,128]{2,1,0:T(8,128)(2,1)S(1)}, u32[]{:S(2)}, u32[]{:S(2)}) collective-permute-start(bf16[2,64,128]{2,1,0:T(8,128)(2,1)S(1)} %get-tuple-element.28), channel_id=1, source_target_pairs={{0,4},{8,12},{16,20},{24,28},{4,0},{12,8},{20,16},{28,24},{1,5},{9... | collective-permute-start | bytes 98312 | tf_op jit(solution)/shard_map/ppermute | solution.py:298
  8.2 0.7 %copy-start.4 = (s32[4,27]{1,0:T(4,128)S(1)}, s32[4,27]{1,0:T(4,128)}, u32[]{:S(2)}) copy-start(s32[4,27]{1,0:T(4,128)} %param.7) | copy-start | bytes 1300
  9.0 1.0 %copy-start.2 = (bf16[27,64,64]{2,1,0:T(8,128)(2,1)S(1)}, bf16[27,64,64]{2,1,0:T(8,128)(2,1)}, u32[]{:S(2)}) copy-start(bf16[27,64,64]{2,1,0:T(8,128)(2,1)} %cw_ref.1) | copy-start | bytes 663556
  10.0 0.9 %copy-start = (bf16[4,64,512]{2,1,0:T(8,128)(2,1)S(1)}, bf16[4,64,512]{2,1,0:T(8,128)(2,1)}, u32[]{:S(2)}) copy-start(bf16[4,64,512]{2,1,0:T(8,128)(2,1)} %feat_ref.1) | copy-start | bytes 786436
  14.6 1.5 %collective-permute-start.2 = (f32[352,128]{1,0:T(8,128)S(1)}, f32[352,128]{1,0:T(8,128)S(1)}, u32[]{:S(2)}, u32[]{:S(2)}) collective-permute-start(f32[352,128]{1,0:T(8,128)S(1)} %get-tuple-element.18), channel_id=1, source_target_pairs={{0,1},{1,0},{2,3},{3,2},{4,5},{5,4},{6,7},{7,6},{8,9},{9,8},{10,11... | collective-permute-start | bytes 540680 | tf_op jit(solution)/shard_map/ppermute | solution.py:251
  14.7 3.0 %collective-permute-start.9 = (f32[352,128]{1,0:T(8,128)S(1)}, f32[352,128]{1,0:T(8,128)S(1)}, u32[]{:S(2)}, u32[]{:S(2)}) collective-permute-start(f32[352,128]{1,0:T(8,128)S(1)} %get-tuple-element.20), channel_id=1, source_target_pairs={{0,1},{1,0},{2,3},{3,2},{4,5},{5,4},{6,7},{7,6},{8,9},{9,8},{10,11... | collective-permute-start | bytes 540680 | tf_op jit(solution)/shard_map/ppermute | solution.py:251
  16.2 4.6 %collective-permute-start.3 = (f32[176,128]{1,0:T(8,128)S(1)}, f32[176,128]{1,0:T(8,128)S(1)}, u32[]{:S(2)}, u32[]{:S(2)}) collective-permute-start(f32[176,128]{1,0:T(8,128)S(1)} %slice_select_fusion.1), channel_id=1, source_target_pairs={{0,2},{1,5},{2,0},{3,7},{4,6},{5,1},{6,4},{7,3},{8,10},{9,13},{10,... | collective-permute-start | bytes 270344 | tf_op jit(solution)/shard_map/ppermute | solution.py:262
  17.8 4.6 %collective-permute-start.10 = (f32[176,128]{1,0:T(8,128)S(1)}, f32[176,128]{1,0:T(8,128)S(1)}, u32[]{:S(2)}, u32[]{:S(2)}) collective-permute-start(f32[176,128]{1,0:T(8,128)S(1)} %slice_select_fusion), channel_id=1, source_target_pairs={{0,2},{1,5},{2,0},{3,7},{4,6},{5,1},{6,4},{7,3},{8,10},{9,13},{10,... | collective-permute-start | bytes 270344 | tf_op jit(solution)/shard_map/ppermute | solution.py:262
  20.8 4.6 %collective-permute-start.4 = (f32[176,128]{1,0:T(8,128)S(1)}, f32[176,128]{1,0:T(8,128)S(1)}, u32[]{:S(2)}, u32[]{:S(2)}) collective-permute-start(f32[176,128]{1,0:T(8,128)S(1)} %select_add_fusion.1), channel_id=1, source_target_pairs={{0,4},{1,3},{2,6},{3,1},{4,0},{5,7},{6,2},{7,5},{8,12},{9,11},{10,... | collective-permute-start | bytes 270344 | tf_op jit(solution)/shard_map/ppermute | solution.py:262
  22.4 4.7 %collective-permute-start.11 = (f32[176,128]{1,0:T(8,128)S(1)}, f32[176,128]{1,0:T(8,128)S(1)}, u32[]{:S(2)}, u32[]{:S(2)}) collective-permute-start(f32[176,128]{1,0:T(8,128)S(1)} %select_add_fusion), channel_id=1, source_target_pairs={{0,4},{1,3},{2,6},{3,1},{4,0},{5,7},{6,2},{7,5},{8,12},{9,11},{10,... | collective-permute-start | bytes 270344 | tf_op jit(solution)/shard_map/ppermute | solution.py:262
  25.4 5.1 %collective-permute-start.5 = (f32[176,128]{1,0:T(8,128)S(1)}, f32[176,128]{1,0:T(8,128)S(1)}, u32[]{:S(2)}, u32[]{:S(2)}) collective-permute-start(f32[176,128]{1,0:T(8,128)S(1)} %add.32), channel_id=1, source_target_pairs={{0,8},{1,17},{2,10},{3,19},{4,12},{5,21},{6,14},{7,23},{8,0},{9,25... | collective-permute-start | bytes 270344 | tf_op jit(solution)/shard_map/ppermute | solution.py:262
  27.1 5.8 %collective-permute-start.12 = (f32[176,128]{1,0:T(8,128)S(1)}, f32[176,128]{1,0:T(8,128)S(1)}, u32[]{:S(2)}, u32[]{:S(2)}) collective-permute-start(f32[176,128]{1,0:T(8,128)S(1)} %add.37), channel_id=1, source_target_pairs={{0,8},{1,17},{2,10},{3,19},{4,12},{5,21},{6,14},{7,23},{8,0},{9,25... | collective-permute-start | bytes 270344 | tf_op jit(solution)/shard_map/ppermute | solution.py:262
  30.6 5.5 %collective-permute-start.6 = (f32[176,128]{1,0:T(8,128)S(1)}, f32[176,128]{1,0:T(8,128)S(1)}, u32[]{:S(2)}, u32[]{:S(2)}) collective-permute-start(f32[176,128]{1,0:T(8,128)S(1)} %add.33), channel_id=1, source_target_pairs={{0,16},{1,9},{2,18},{3,11},{4,20},{5,13},{6,22},{7,15},{8,24},{9,1... | collective-permute-start | bytes 270344 | tf_op jit(solution)/shard_map/ppermute | solution.py:262
  32.9 5.5 %collective-permute-start.13 = (f32[176,128]{1,0:T(8,128)S(1)}, f32[176,128]{1,0:T(8,128)S(1)}, u32[]{:S(2)}, u32[]{:S(2)}) collective-permute-start(f32[176,128]{1,0:T(8,128)S(1)} %add.38), channel_id=1, source_target_pairs={{0,16},{1,9},{2,18},{3,11},{4,20},{5,13},{6,22},{7,15},{8,24},{9,1... | collective-permute-start | bytes 270344 | tf_op jit(solution)/shard_map/ppermute | solution.py:262
  36.1 4.6 %collective-permute-start.7 = (f32[176,128]{1,0:T(8,128)S(1)}, f32[176,128]{1,0:T(8,128)S(1)}, u32[]{:S(2)}, u32[]{:S(2)}) collective-permute-start(f32[176,128]{1,0:T(8,128)S(1)} %add.34), channel_id=1, source_target_pairs={{0,2},{1,5},{2,0},{3,7},{4,6},{5,1},{6,4},{7,3},{8,10},{9,13},{10,... | collective-permute-start | bytes 270344 | tf_op jit(solution)/shard_map/ppermute | solution.py:262
  38.4 4.6 %collective-permute-start.14 = (f32[176,128]{1,0:T(8,128)S(1)}, f32[176,128]{1,0:T(8,128)S(1)}, u32[]{:S(2)}, u32[]{:S(2)}) collective-permute-start(f32[176,128]{1,0:T(8,128)S(1)} %add.39), channel_id=1, source_target_pairs={{0,2},{1,5},{2,0},{3,7},{4,6},{5,1},{6,4},{7,3},{8,10},{9,13},{10,... | collective-permute-start | bytes 270344 | tf_op jit(solution)/shard_map/ppermute | solution.py:262
  40.7 2.4 %collective-permute-start.8 = (f32[352,128]{1,0:T(8,128)S(1)}, f32[352,128]{1,0:T(8,128)S(1)}, u32[]{:S(2)}, u32[]{:S(2)}) collective-permute-start(f32[352,128]{1,0:T(8,128)S(1)} %maximum_select_fusion.mine_a), channel_id=1, source_target_pairs={{0,1},{1,0},{2,3},{3,2},{4,5},{5,4},{6,7},{7,6},{8,9},{9,8},{10,11... | collective-permute-start | bytes 540680 | tf_op jit(solution)/shard_map/ppermute | solution.py:251
  43.0 1.5 %collective-permute-start.15 = (f32[352,128]{1,0:T(8,128)S(1)}, f32[352,128]{1,0:T(8,128)S(1)}, u32[]{:S(2)}, u32[]{:S(2)}) collective-permute-start(f32[352,128]{1,0:T(8,128)S(1)} %maximum_select_fusion.1.mine_b), channel_id=1, source_target_pairs={{0,1},{1,0},{2,3},{3,2},{4,5},{5,4},{6,7},{7,6},{8,9},{9,8},{10,11... | collective-permute-start | bytes 540680 | tf_op jit(solution)/shard_map/ppermute | solution.py:251
